TPU v7x, 32 devices: a whole 2x2x4 slice. The times are simulated.
32 devices in a mesh: groups: 2 (over x), depth: 16 (over z, y, core).
Axes of the slice: x: 2, y: 2, z: 4, core: 2. Of those that a mesh axis runs over, the one named last changes fastest.
Arguments:
- object_slices: bfloat16 [32, 2, 512, 512], P(('groups', 'depth')), parts along dimension 0, may hold values from -1 to 1, as said below
- probes: float32 [8, 2, 128, 128], P('groups'), parts along dimension 0, may hold values from -4 to 4
- measured: float32 [16, 128, 128], P('groups'), parts along dimension 0, may hold values from 0.05 to 5
- scan_offsets: int32 [16, 2], P('groups'), parts along dimension 0, may hold values from 0 to 384
- probe_ids: int32 [16], P('groups'), parts along dimension 0, may hold values from 0 to 3
Outputs:
- object_grad: bfloat16 [32, 2, 512, 512], P(('groups', 'depth')), parts along dimension 0
There are 2 independent parts, one for each index of `groups`. A program takes and returns all parts, laid end to end along the dimension named above; each array names one. Nothing has to cross between parts.
Inputs may be any that keep to these rules, and one draw needn't show every extreme that they name: `scan_offsets`: row and column of the first pixel of each position's window in the object. `probe_ids`: the probe state used at each position. `object_slices`: real and imaginary parts of a transmission whose modulus is at most 1.
All inputs are finite; a program needn't handle non-finite values.
Results may differ from a plain program's by a relative error of at most 0.001.
Values sent between devices are 32-bit elements; how exact they have to be, the bound alone decides.
A program may use at most 64 MiB of HBM per device.

v0:
```python
import math

import jax
import jax.numpy as jnp
from jax import lax
from jax.sharding import PartitionSpec as P


def shifted(x, axis, by):
    peers = lax.axis_size(axis)
    pairs = [(i, i + by) for i in range(peers) if 0 <= i + by < peers]
    return lax.ppermute(x, axis, pairs)


def dft_tables(length):
    ordinal = jnp.arange(length, dtype=jnp.int32)
    products = ordinal[:, None] * ordinal[None, :] % length
    phase_angle = products.astype(jnp.float32) * (2.0 * math.pi / length)
    factor = 1.0 / math.sqrt(length)
    return (jnp.cos(phase_angle) * factor, -jnp.sin(phase_angle) * factor)


def kernel_table(length):
    ordinal = jnp.arange(length, dtype=jnp.int32)
    spatial = jnp.where(ordinal < length // 2, ordinal, ordinal - length)
    squares = (spatial[:, None] * spatial[:, None] + spatial[None, :] * spatial[None, :]) % (
        2 * length
    )
    phase_angle = squares.astype(jnp.float32) * (math.pi / length)
    return (jnp.cos(phase_angle), -jnp.sin(phase_angle))


def matmul_last(values, table):
    return jnp.einsum("bxk,kc->bxc", values, table, precision=lax.Precision.HIGHEST)


def matmul_first(table, values):
    return jnp.einsum("rj,bjc->brc", table, values, precision=lax.Precision.HIGHEST)


def transform(field_in, table_real, table_imag):
    real_part = field_in[:, 0]
    imag_part = field_in[:, 1]
    mid_real = matmul_last(real_part, table_real) - matmul_last(imag_part, table_imag)
    mid_imag = matmul_last(real_part, table_imag) + matmul_last(imag_part, table_real)
    out_real = matmul_first(table_real, mid_real) - matmul_first(table_imag, mid_imag)
    out_imag = matmul_first(table_real, mid_imag) + matmul_first(table_imag, mid_real)
    return (out_real, out_imag)


def complex_mul(left_real, left_imag, right_real, right_imag):
    return (
        left_real * right_real - left_imag * right_imag,
        left_real * right_imag + left_imag * right_real,
    )


def cut_windows(object_slab, corners, window):
    zero_index = jnp.zeros((), jnp.int32)

    def one_window(corner):
        return lax.dynamic_slice(
            object_slab, (zero_index, corner[0], corner[1]), (2, window, window)
        )

    return jax.vmap(one_window)(corners)


def send_forward(message):
    return shifted(message, "depth", 1)


def send_backward(message):
    return shifted(message, "depth", -1)


def body(object_slices, probes, measured, scan_offsets, probe_ids):
    depth_count = lax.axis_size("depth")
    depth_index = lax.axis_index("depth")
    window = probes.shape[-1]
    object_side = object_slices.shape[-1]
    position_count = scan_offsets.shape[0]
    probe_count = probes.shape[0]
    table_real, table_imag = dft_tables(window)
    kernel_real, kernel_imag = kernel_table(window)
    is_first = depth_index == 0
    is_last = depth_index == depth_count - 1
    group_size = 1
    group_count = position_count // group_size
    object_slab = object_slices[0]
    probe_slots = jnp.arange(probe_count, dtype=jnp.int32)
    zero_index = jnp.zeros((), jnp.int32)
    blank_wave = jnp.zeros((group_size, 2, window, window), jnp.float32)

    def propagate(field_in, kernel_sign):
        spec_real, spec_imag = transform(field_in, table_real, table_imag)
        mixed_real, mixed_imag = complex_mul(
            spec_real, spec_imag, kernel_real, kernel_sign * kernel_imag
        )
        mixed_wave = jnp.stack([mixed_real, mixed_imag], 1)
        return transform(mixed_wave, table_real, -table_imag)

    def group_rows(micro_at):
        first_row = micro_at * group_size
        corners = lax.dynamic_slice_in_dim(scan_offsets, first_row, group_size, 0)
        chosen_ids = lax.dynamic_slice_in_dim(probe_ids, first_row, group_size, 0)
        matches = chosen_ids[:, None] == probe_slots[None, :]
        return (first_row, corners, matches)

    def forward_work(carried, incoming, micro_at):
        stored_in, far_grad, grad_sum = carried
        first_row, corners, matches = group_rows(micro_at)
        picked = jnp.sum(jnp.where(matches[:, :, None, None, None], probes[None], 0.0), axis=1)
        wave_in = jnp.where(is_first, picked, incoming)
        stored_in = lax.dynamic_update_slice_in_dim(stored_in, wave_in, first_row, 0)
        windows = cut_windows(object_slab, corners, window).astype(jnp.float32)
        exit_real, exit_imag = complex_mul(
            wave_in[:, 0], wave_in[:, 1], windows[:, 0], windows[:, 1]
        )
        exit_wave = jnp.stack([exit_real, exit_imag], 1)
        spec_real, spec_imag = transform(exit_wave, table_real, table_imag)

        def far_field():
            target = lax.dynamic_slice_in_dim(measured, first_row, group_size, 0)
            excess = spec_real * spec_real + spec_imag * spec_imag - target
            residue = jnp.stack([excess * spec_real, excess * spec_imag], 1)
            seed_real, seed_imag = transform(residue, table_real, -table_imag)
            seed_wave = jnp.stack([seed_real, seed_imag], 1)
            return (lax.dynamic_update_slice_in_dim(far_grad, seed_wave, first_row, 0), blank_wave)

        def onward():
            mixed_real, mixed_imag = complex_mul(spec_real, spec_imag, kernel_real, kernel_imag)
            mixed_wave = jnp.stack([mixed_real, mixed_imag], 1)
            out_real, out_imag = transform(mixed_wave, table_real, -table_imag)
            return (far_grad, jnp.stack([out_real, out_imag], 1))

        far_grad, outgoing = lax.cond(is_last, far_field, onward)
        return ((stored_in, far_grad, grad_sum), outgoing)

    def backward_work(carried, incoming, micro_at):
        stored_in, far_grad, grad_sum = carried
        first_row, corners, unused_matches = group_rows(micro_at)

        def from_far():
            return lax.dynamic_slice_in_dim(far_grad, first_row, group_size, 0)

        def from_next():
            prev_real, prev_imag = propagate(incoming, -1.0)
            return jnp.stack([prev_real, prev_imag], 1)

        back_wave = lax.cond(is_last, from_far, from_next)
        wave_full = lax.dynamic_slice_in_dim(stored_in, first_row, group_size, 0)
        windows = cut_windows(object_slab, corners, window).astype(jnp.float32)
        term_real = wave_full[:, 0] * back_wave[:, 0] + wave_full[:, 1] * back_wave[:, 1]
        term_imag = wave_full[:, 0] * back_wave[:, 1] - wave_full[:, 1] * back_wave[:, 0]
        grad_term = jnp.stack([term_real, term_imag], 1)
        corner_at = (zero_index, corners[0, 0], corners[0, 1])
        current = lax.dynamic_slice(grad_sum, corner_at, (2, window, window))
        grad_sum = lax.dynamic_update_slice(grad_sum, current + grad_term[0], corner_at)
        sent_real = windows[:, 0] * back_wave[:, 0] + windows[:, 1] * back_wave[:, 1]
        sent_imag = windows[:, 0] * back_wave[:, 1] - windows[:, 1] * back_wave[:, 0]
        sent_wave = jnp.stack([sent_real, sent_imag], 1)
        return ((stored_in, far_grad, grad_sum), sent_wave)

    def guarded(work, carried, incoming, micro_at):
        valid = (micro_at >= 0) & (micro_at < group_count)
        clipped = jnp.clip(micro_at, 0, group_count - 1)
        return lax.cond(
            valid, lambda: work(carried, incoming, clipped), lambda: (carried, blank_wave)
        )

    initial = (
        jnp.zeros((position_count, 2, window, window), jnp.float32),
        jnp.zeros((position_count, 2, window, window), jnp.float32),
        jnp.zeros((2, object_side, object_side), jnp.float32),
    )

    def forward_step(step_at, loop_state):
        carried, forward_msg = loop_state
        carried, forward_out = guarded(forward_work, carried, forward_msg, step_at - depth_index)
        return (carried, send_forward(forward_out))

    def backward_step(step_at, loop_state):
        carried, backward_msg = loop_state
        carried, backward_out = guarded(
            backward_work, carried, backward_msg, step_at - (depth_count - 1 - depth_index)
        )
        return (carried, send_backward(backward_out))

    carried, unused_forward = lax.fori_loop(
        0, depth_count + group_count - 1, forward_step, (initial, blank_wave)
    )
    carried, unused_backward = lax.fori_loop(
        0, depth_count + group_count - 1, backward_step, (carried, blank_wave)
    )
    grad_sum = carried[2]
    return grad_sum.astype(jnp.bfloat16)[None]


def solution(mesh):
    return jax.shard_map(
        body,
        mesh=mesh,
        in_specs=(
            P(("groups", "depth"), None, None, None),
            P("groups", None, None, None),
            P("groups", None, None),
            P("groups", None),
            P("groups"),
        ),
        out_specs=P(("groups", "depth"), None, None, None),
        check_vma=False,
    )
```

profile of v0, /device:TPU:0, one launch (start us, length us, event | category | flops | bytes accessed | tf_op | source)
XLA Modules:
  0.0 1017.1 jit_solution(5227656086588721411)
XLA Ops:
  2.6 334.4 %while.45 = (s32[]{:T(128)}, f32[8,2,128,128]{3,2,1,0:T(8,128)S(1)}, f32[8,2,128,128]{2,3,1,0:T(8,128)S(1)}, f32[1,2,128,128]{3,2,1,0:T(8,128)S(1)}, s32[]{:T(12...) while((s32[]{:T(128)}, ...), condition=%wide.region_6.7_spmd.clone.clone.clone, body=%wide.region_0.6_spmd.clone.clone.clone.sunk | while | flops 403898368 | bytes 8127841 | solution.py:190
  2.8 12.8 %conditional.14 = (f32[8,2,128,128]{3,2,1,0:T(8,128)S(1)}, f32[8,2,128,128]{2,3,1,0:T(8,128)S(1)}, f32[1,2,128,128]{3,2,1,0:T(8,128)}) conditional(s32[]{:T(128)} %convert_element_type.221, (f32[8,2,128,128]{3,2,1,0:T(8,128)S(1)}, f32[8,2,128,128]{2,3,1,0:T(8,128)S(1)}) %tuple.218, (pred[]{:T(512)}, s32[]{:T(128)}, s32[8]{0:T(128)S(1)}, ...), branch_computations={%region_1.1_spmd, %region_2.5_spmd.clone} | conditional | flops 403439616 | bytes 7406018 | solution.py:168
  18.2 12.8 %conditional.14 = (f32[8,2,128,128]{3,2,1,0:T(8,128)S(1)}, f32[8,2,128,128]{2,3,1,0:T(8,128)S(1)}, f32[1,2,128,128]{3,2,1,0:T(8,128)}) conditional(s32[]{:T(128)} %convert_element_type.221, (f32[8,2,128,128]{3,2,1,0:T(8,128)S(1)}, f32[8,2,128,128]{2,3,1,0:T(8,128)S(1)}) %tuple.218, (pred[]{:T(512)}, s32[]{:T(128)}, s32[8]{0:T(128)S(1)}, ...), branch_computations={%region_1.1_spmd, %region_2.5_spmd.clone} | conditional | flops 403439616 | bytes 7406018 | solution.py:168
  34.6 12.8 %conditional.14 = (f32[8,2,128,128]{3,2,1,0:T(8,128)S(1)}, f32[8,2,128,128]{2,3,1,0:T(8,128)S(1)}, f32[1,2,128,128]{3,2,1,0:T(8,128)}) conditional(s32[]{:T(128)} %convert_element_type.221, (f32[8,2,128,128]{3,2,1,0:T(8,128)S(1)}, f32[8,2,128,128]{2,3,1,0:T(8,128)S(1)}) %tuple.218, (pred[]{:T(512)}, s32[]{:T(128)}, s32[8]{0:T(128)S(1)}, ...), branch_computations={%region_1.1_spmd, %region_2.5_spmd.clone} | conditional | flops 403439616 | bytes 7406018 | solution.py:168
  51.7 12.8 %conditional.14 = (f32[8,2,128,128]{3,2,1,0:T(8,128)S(1)}, f32[8,2,128,128]{2,3,1,0:T(8,128)S(1)}, f32[1,2,128,128]{3,2,1,0:T(8,128)}) conditional(s32[]{:T(128)} %convert_element_type.221, (f32[8,2,128,128]{3,2,1,0:T(8,128)S(1)}, f32[8,2,128,128]{2,3,1,0:T(8,128)S(1)}) %tuple.218, (pred[]{:T(512)}, s32[]{:T(128)}, s32[8]{0:T(128)S(1)}, ...), branch_computations={%region_1.1_spmd, %region_2.5_spmd.clone} | conditional | flops 403439616 | bytes 7406018 | solution.py:168
  71.1 12.8 %conditional.14 = (f32[8,2,128,128]{3,2,1,0:T(8,128)S(1)}, f32[8,2,128,128]{2,3,1,0:T(8,128)S(1)}, f32[1,2,128,128]{3,2,1,0:T(8,128)}) conditional(s32[]{:T(128)} %convert_element_type.221, (f32[8,2,128,128]{3,2,1,0:T(8,128)S(1)}, f32[8,2,128,128]{2,3,1,0:T(8,128)S(1)}) %tuple.218, (pred[]{:T(512)}, s32[]{:T(128)}, s32[8]{0:T(128)S(1)}, ...), branch_computations={%region_1.1_spmd, %region_2.5_spmd.clone} | conditional | flops 403439616 | bytes 7406018 | solution.py:168
  90.5 12.8 %conditional.14 = (f32[8,2,128,128]{3,2,1,0:T(8,128)S(1)}, f32[8,2,128,128]{2,3,1,0:T(8,128)S(1)}, f32[1,2,128,128]{3,2,1,0:T(8,128)}) conditional(s32[]{:T(128)} %convert_element_type.221, (f32[8,2,128,128]{3,2,1,0:T(8,128)S(1)}, f32[8,2,128,128]{2,3,1,0:T(8,128)S(1)}) %tuple.218, (pred[]{:T(512)}, s32[]{:T(128)}, s32[8]{0:T(128)S(1)}, ...), branch_computations={%region_1.1_spmd, %region_2.5_spmd.clone} | conditional | flops 403439616 | bytes 7406018 | solution.py:168
  110.0 12.8 %conditional.14 = (f32[8,2,128,128]{3,2,1,0:T(8,128)S(1)}, f32[8,2,128,128]{2,3,1,0:T(8,128)S(1)}, f32[1,2,128,128]{3,2,1,0:T(8,128)}) conditional(s32[]{:T(128)} %convert_element_type.221, (f32[8,2,128,128]{3,2,1,0:T(8,128)S(1)}, f32[8,2,128,128]{2,3,1,0:T(8,128)S(1)}) %tuple.218, (pred[]{:T(512)}, s32[]{:T(128)}, s32[8]{0:T(128)S(1)}, ...), branch_computations={%region_1.1_spmd, %region_2.5_spmd.clone} | conditional | flops 403439616 | bytes 7406018 | solution.py:168
  129.4 12.8 %conditional.14 = (f32[8,2,128,128]{3,2,1,0:T(8,128)S(1)}, f32[8,2,128,128]{2,3,1,0:T(8,128)S(1)}, f32[1,2,128,128]{3,2,1,0:T(8,128)}) conditional(s32[]{:T(128)} %convert_element_type.221, (f32[8,2,128,128]{3,2,1,0:T(8,128)S(1)}, f32[8,2,128,128]{2,3,1,0:T(8,128)S(1)}) %tuple.218, (pred[]{:T(512)}, s32[]{:T(128)}, s32[8]{0:T(128)S(1)}, ...), branch_computations={%region_1.1_spmd, %region_2.5_spmd.clone} | conditional | flops 403439616 | bytes 7406018 | solution.py:168
  149.5 17.4 %collective-permute-start = (f32[1,2,128,128]{3,2,1,0:T(8,128)}, f32[1,2,128,128]{3,2,1,0:T(8,128)S(1)}, u32[]{:S(2)}, u32[]{:S(2)}) collective-permute-start(f32[1,2,128,128]{3,2,1,0:T(8,128)} %get-tuple-element.1762), channel_id=1, source_target_pairs={{0,1},{1,2},{2,3},{3,4},{4,5},{5,6},{6,7},{7,8},{8,9},{9,10},{10,1... | collective-permute-start | bytes 393224 | tf_op jit(solution)/shard_map/while/body/eval_jaxpr/ppermute | solution.py:12
  176.2 17.4 %collective-permute-start = (f32[1,2,128,128]{3,2,1,0:T(8,128)}, f32[1,2,128,128]{3,2,1,0:T(8,128)S(1)}, u32[]{:S(2)}, u32[]{:S(2)}) collective-permute-start(f32[1,2,128,128]{3,2,1,0:T(8,128)} %get-tuple-element.1762), channel_id=1, source_target_pairs={{0,1},{1,2},{2,3},{3,4},{4,5},{5,6},{6,7},{7,8},{8,9},{9,10},{10,1... | collective-permute-start | bytes 393224 | tf_op jit(solution)/shard_map/while/body/eval_jaxpr/ppermute | solution.py:12
  203.0 14.1 %collective-permute-start = (f32[1,2,128,128]{3,2,1,0:T(8,128)}, f32[1,2,128,128]{3,2,1,0:T(8,128)S(1)}, u32[]{:S(2)}, u32[]{:S(2)}) collective-permute-start(f32[1,2,128,128]{3,2,1,0:T(8,128)} %get-tuple-element.1762), channel_id=1, source_target_pairs={{0,1},{1,2},{2,3},{3,4},{4,5},{5,6},{6,7},{7,8},{8,9},{9,10},{10,1... | collective-permute-start | bytes 393224 | tf_op jit(solution)/shard_map/while/body/eval_jaxpr/ppermute | solution.py:12
  219.0 6.2 collective-permute-start
  227.2 18.3 %collective-permute-start = (f32[1,2,128,128]{3,2,1,0:T(8,128)}, f32[1,2,128,128]{3,2,1,0:T(8,128)S(1)}, u32[]{:S(2)}, u32[]{:S(2)}) collective-permute-start(f32[1,2,128,128]{3,2,1,0:T(8,128)} %get-tuple-element.1762), channel_id=1, source_target_pairs={{0,1},{1,2},{2,3},{3,4},{4,5},{5,6},{6,7},{7,8},{8,9},{9,10},{10,1... | collective-permute-start | bytes 393224 | tf_op jit(solution)/shard_map/while/body/eval_jaxpr/ppermute | solution.py:12
  247.6 6.2 collective-permute-start
  255.8 10.1 collective-permute-start
  267.9 6.2 collective-permute-start
  276.0 14.2 %collective-permute-start = (f32[1,2,128,128]{3,2,1,0:T(8,128)}, f32[1,2,128,128]{3,2,1,0:T(8,128)S(1)}, u32[]{:S(2)}, u32[]{:S(2)}) collective-permute-start(f32[1,2,128,128]{3,2,1,0:T(8,128)} %get-tuple-element.1762), channel_id=1, source_target_pairs={{0,1},{1,2},{2,3},{3,4},{4,5},{5,6},{6,7},{7,8},{8,9},{9,10},{10,1... | collective-permute-start | bytes 393224 | tf_op jit(solution)/shard_map/while/body/eval_jaxpr/ppermute | solution.py:12
  292.3 6.2 collective-permute-start
  300.4 10.1 collective-permute-start
  312.5 6.2 collective-permute-start
  320.7 15.1 %collective-permute-start = (f32[1,2,128,128]{3,2,1,0:T(8,128)}, f32[1,2,128,128]{3,2,1,0:T(8,128)S(1)}, u32[]{:S(2)}, u32[]{:S(2)}) collective-permute-start(f32[1,2,128,128]{3,2,1,0:T(8,128)} %get-tuple-element.1762), channel_id=1, source_target_pairs={{0,1},{1,2},{2,3},{3,4},{4,5},{5,6},{6,7},{7,8},{8,9},{9,10},{10,1... | collective-permute-start | bytes 393224 | tf_op jit(solution)/shard_map/while/body/eval_jaxpr/ppermute | solution.py:12
  340.3 674.2 %while.46 = (s32[]{:T(128)}, f32[2,512,512]{1,2,0:T(8,128)}, f32[1,2,128,128]{2,3,1,0:T(8,128)S(1)}, s32[]{:T(128)}, s32[8,2]{0,1:T(2,128)S(1)}, /*index=5*/f32[...) while((s32[]{:T(128)}, f32[2,512,512]{1,2,0:T(8,128)}, ...), condition=%wide.region_12.13_spmd.clone.clone.clone, body=%wide.region_7.12_spmd.clone.clone.clone.sunk | while | flops 403832832 | bytes 7472400 | solution.py:193
  349.1 10.4 %collective-permute-done.1 = f32[1,2,128,128]{2,3,1,0:T(8,128)S(1)} collective-permute-done((f32[1,2,128,128]{2,3,1,0:T(8,128)S(1)}, f32[1,2,128,128]{2,3,1,0:T(8,128)S(1)}, u32[]{:S(2)}, u32[]{:S(2)}) %collective-permute-start.1) | collective-permute-done | bytes 131104 | tf_op jit(solution)/shard_map/while/body/eval_jaxpr/ppermute | solution.py:12
  368.3 14.5 %collective-permute-done.1 = f32[1,2,128,128]{2,3,1,0:T(8,128)S(1)} collective-permute-done((f32[1,2,128,128]{2,3,1,0:T(8,128)S(1)}, f32[1,2,128,128]{2,3,1,0:T(8,128)S(1)}, u32[]{:S(2)}, u32[]{:S(2)}) %collective-permute-start.1) | collective-permute-done | bytes 131104 | tf_op jit(solution)/shard_map/while/body/eval_jaxpr/ppermute | solution.py:12
  384.3 5.9 collective-permute-done.1
  391.7 10.3 %collective-permute-done.1 = f32[1,2,128,128]{2,3,1,0:T(8,128)S(1)} collective-permute-done((f32[1,2,128,128]{2,3,1,0:T(8,128)S(1)}, f32[1,2,128,128]{2,3,1,0:T(8,128)S(1)}, u32[]{:S(2)}, u32[]{:S(2)}) %collective-permute-start.1) | collective-permute-done | bytes 131104 | tf_op jit(solution)/shard_map/while/body/eval_jaxpr/ppermute | solution.py:12
  403.5 5.9 collective-permute-done.1
  410.9 15.3 %collective-permute-done.1 = f32[1,2,128,128]{2,3,1,0:T(8,128)S(1)} collective-permute-done((f32[1,2,128,128]{2,3,1,0:T(8,128)S(1)}, f32[1,2,128,128]{2,3,1,0:T(8,128)S(1)}, u32[]{:S(2)}, u32[]{:S(2)}) %collective-permute-start.1) | collective-permute-done | bytes 131104 | tf_op jit(solution)/shard_map/while/body/eval_jaxpr/ppermute | solution.py:12
  427.7 5.9 collective-permute-done.1
  435.1 10.3 %collective-permute-done.1 = f32[1,2,128,128]{2,3,1,0:T(8,128)S(1)} collective-permute-done((f32[1,2,128,128]{2,3,1,0:T(8,128)S(1)}, f32[1,2,128,128]{2,3,1,0:T(8,128)S(1)}, u32[]{:S(2)}, u32[]{:S(2)}) %collective-permute-start.1) | collective-permute-done | bytes 131104 | tf_op jit(solution)/shard_map/while/body/eval_jaxpr/ppermute | solution.py:12
  446.9 5.9 collective-permute-done.1
  454.3 14.4 %collective-permute-done.1 = f32[1,2,128,128]{2,3,1,0:T(8,128)S(1)} collective-permute-done((f32[1,2,128,128]{2,3,1,0:T(8,128)S(1)}, f32[1,2,128,128]{2,3,1,0:T(8,128)S(1)}, u32[]{:S(2)}, u32[]{:S(2)}) %collective-permute-start.1) | collective-permute-done | bytes 131104 | tf_op jit(solution)/shard_map/while/body/eval_jaxpr/ppermute | solution.py:12
  470.1 5.9 collective-permute-done.1
  477.6 11.0 %collective-permute-done.1 = f32[1,2,128,128]{2,3,1,0:T(8,128)S(1)} collective-permute-done((f32[1,2,128,128]{2,3,1,0:T(8,128)S(1)}, f32[1,2,128,128]{2,3,1,0:T(8,128)S(1)}, u32[]{:S(2)}, u32[]{:S(2)}) %collective-permute-start.1) | collective-permute-done | bytes 131104 | tf_op jit(solution)/shard_map/while/body/eval_jaxpr/ppermute | solution.py:12
  490.1 306.5 %collective-permute-done.1 = f32[1,2,128,128]{2,3,1,0:T(8,128)S(1)} collective-permute-done((f32[1,2,128,128]{2,3,1,0:T(8,128)S(1)}, f32[1,2,128,128]{2,3,1,0:T(8,128)S(1)}, u32[]{:S(2)}, u32[]{:S(2)}) %collective-permute-start.1) | collective-permute-done | bytes 131104 | tf_op jit(solution)/shard_map/while/body/eval_jaxpr/ppermute | solution.py:12
  796.8 20.7 %conditional.15 = (f32[2,512,512]{1,2,0:T(8,128)}, f32[1,2,128,128]{2,3,1,0:T(8,128)S(1)}) conditional(s32[]{:T(128)} %convert_element_type.224, f32[2,512,512]{1,2,0:T(8,128)} %get-tuple-element.1859, (s32[]{:T(128)}, s32[8,2]{0,1:T(2,128)S(1)}, f32[2,512,512]{1,2,0:T(8,128)}, f32[8,2,128,128]{2,3,1,0:T(8,128)}, pred[]{:T(512)}, ...), branch_computations={%region_8.8_spmd, %region_9.11_spmd.clone} | conditional | flops 403374080 | bytes 6750665 | solution.py:168
  818.7 5.8 collective-permute-done.1
  824.8 20.7 %conditional.15 = (f32[2,512,512]{1,2,0:T(8,128)}, f32[1,2,128,128]{2,3,1,0:T(8,128)S(1)}) conditional(s32[]{:T(128)} %convert_element_type.224, f32[2,512,512]{1,2,0:T(8,128)} %get-tuple-element.1859, (s32[]{:T(128)}, s32[8,2]{0,1:T(2,128)S(1)}, f32[2,512,512]{1,2,0:T(8,128)}, f32[8,2,128,128]{2,3,1,0:T(8,128)}, pred[]{:T(512)}, ...), branch_computations={%region_8.8_spmd, %region_9.11_spmd.clone} | conditional | flops 403374080 | bytes 6750665 | solution.py:168
  851.9 20.4 %conditional.15 = (f32[2,512,512]{1,2,0:T(8,128)}, f32[1,2,128,128]{2,3,1,0:T(8,128)S(1)}) conditional(s32[]{:T(128)} %convert_element_type.224, f32[2,512,512]{1,2,0:T(8,128)} %get-tuple-element.1859, (s32[]{:T(128)}, s32[8,2]{0,1:T(2,128)S(1)}, f32[2,512,512]{1,2,0:T(8,128)}, f32[8,2,128,128]{2,3,1,0:T(8,128)}, pred[]{:T(512)}, ...), branch_computations={%region_8.8_spmd, %region_9.11_spmd.clone} | conditional | flops 403374080 | bytes 6750665 | solution.py:168
  873.6 6.8 collective-permute-done.1
  880.5 20.7 %conditional.15 = (f32[2,512,512]{1,2,0:T(8,128)}, f32[1,2,128,128]{2,3,1,0:T(8,128)S(1)}) conditional(s32[]{:T(128)} %convert_element_type.224, f32[2,512,512]{1,2,0:T(8,128)} %get-tuple-element.1859, (s32[]{:T(128)}, s32[8,2]{0,1:T(2,128)S(1)}, f32[2,512,512]{1,2,0:T(8,128)}, f32[8,2,128,128]{2,3,1,0:T(8,128)}, pred[]{:T(512)}, ...), branch_computations={%region_8.8_spmd, %region_9.11_spmd.clone} | conditional | flops 403374080 | bytes 6750665 | solution.py:168
  902.5 5.9 collective-permute-done.1
  908.6 20.7 %conditional.15 = (f32[2,512,512]{1,2,0:T(8,128)}, f32[1,2,128,128]{2,3,1,0:T(8,128)S(1)}) conditional(s32[]{:T(128)} %convert_element_type.224, f32[2,512,512]{1,2,0:T(8,128)} %get-tuple-element.1859, (s32[]{:T(128)}, s32[8,2]{0,1:T(2,128)S(1)}, f32[2,512,512]{1,2,0:T(8,128)}, f32[8,2,128,128]{2,3,1,0:T(8,128)}, pred[]{:T(512)}, ...), branch_computations={%region_8.8_spmd, %region_9.11_spmd.clone} | conditional | flops 403374080 | bytes 6750665 | solution.py:168
  935.0 20.0 %conditional.15 = (f32[2,512,512]{1,2,0:T(8,128)}, f32[1,2,128,128]{2,3,1,0:T(8,128)S(1)}) conditional(s32[]{:T(128)} %convert_element_type.224, f32[2,512,512]{1,2,0:T(8,128)} %get-tuple-element.1859, (s32[]{:T(128)}, s32[8,2]{0,1:T(2,128)S(1)}, f32[2,512,512]{1,2,0:T(8,128)}, f32[8,2,128,128]{2,3,1,0:T(8,128)}, pred[]{:T(512)}, ...), branch_computations={%region_8.8_spmd, %region_9.11_spmd.clone} | conditional | flops 403374080 | bytes 6750665 | solution.py:168
  961.0 19.6 %conditional.15 = (f32[2,512,512]{1,2,0:T(8,128)}, f32[1,2,128,128]{2,3,1,0:T(8,128)S(1)}) conditional(s32[]{:T(128)} %convert_element_type.224, f32[2,512,512]{1,2,0:T(8,128)} %get-tuple-element.1859, (s32[]{:T(128)}, s32[8,2]{0,1:T(2,128)S(1)}, f32[2,512,512]{1,2,0:T(8,128)}, f32[8,2,128,128]{2,3,1,0:T(8,128)}, pred[]{:T(512)}, ...), branch_computations={%region_8.8_spmd, %region_9.11_spmd.clone} | conditional | flops 403374080 | bytes 6750665 | solution.py:168
  981.8 8.7 collective-permute-done.1
  990.7 20.6 %conditional.15 = (f32[2,512,512]{1,2,0:T(8,128)}, f32[1,2,128,128]{2,3,1,0:T(8,128)S(1)}) conditional(s32[]{:T(128)} %convert_element_type.224, f32[2,512,512]{1,2,0:T(8,128)} %get-tuple-element.1859, (s32[]{:T(128)}, s32[8,2]{0,1:T(2,128)S(1)}, f32[2,512,512]{1,2,0:T(8,128)}, f32[8,2,128,128]{2,3,1,0:T(8,128)}, pred[]{:T(512)}, ...), branch_computations={%region_8.8_spmd, %region_9.11_spmd.clone} | conditional | flops 403374080 | bytes 6750665 | solution.py:168
  (764 shorter events, 392.1 us)
Async XLA Ops:
  0.0 2.6 copy-start.1
  0.0 2.6 copy-start.2
  15.6 2.5 collective-permute-start
  31.0 3.4 collective-permute-start
  47.4 4.2 collective-permute-start
  64.5 6.5 collective-permute-start
  83.9 6.5 collective-permute-start
  103.4 6.5 collective-permute-start
  122.8 6.5 collective-permute-start
  142.2 6.5 collective-permute-start
  149.5 18.6 %collective-permute-start = (f32[1,2,128,128]{3,2,1,0:T(8,128)}, f32[1,2,128,128]{3,2,1,0:T(8,128)S(1)}, u32[]{:S(2)}, u32[]{:S(2)}) collective-permute-start(f32[1,2,128,128]{3,2,1,0:T(8,128)} %get-tuple-element.1762), channel_id=1, source_target_pairs={{0,1},{1,2},{2,3},{3,4},{4,5},{5,6},{6,7},{7,8},{8,9},{9,10},{10,1... | collective-permute-start | bytes 393224 | tf_op jit(solution)/shard_map/while/body/eval_jaxpr/ppermute | solution.py:12
  169.0 6.5 collective-permute-start
  176.2 18.6 %collective-permute-start = (f32[1,2,128,128]{3,2,1,0:T(8,128)}, f32[1,2,128,128]{3,2,1,0:T(8,128)S(1)}, u32[]{:S(2)}, u32[]{:S(2)}) collective-permute-start(f32[1,2,128,128]{3,2,1,0:T(8,128)} %get-tuple-element.1762), channel_id=1, source_target_pairs={{0,1},{1,2},{2,3},{3,4},{4,5},{5,6},{6,7},{7,8},{8,9},{9,10},{10,1... | collective-permute-start | bytes 393224 | tf_op jit(solution)/shard_map/while/body/eval_jaxpr/ppermute | solution.py:12
  195.7 6.5 collective-permute-start
  203.0 15.2 %collective-permute-start = (f32[1,2,128,128]{3,2,1,0:T(8,128)}, f32[1,2,128,128]{3,2,1,0:T(8,128)S(1)}, u32[]{:S(2)}, u32[]{:S(2)}) collective-permute-start(f32[1,2,128,128]{3,2,1,0:T(8,128)} %get-tuple-element.1762), channel_id=1, source_target_pairs={{0,1},{1,2},{2,3},{3,4},{4,5},{5,6},{6,7},{7,8},{8,9},{9,10},{10,1... | collective-permute-start | bytes 393224 | tf_op jit(solution)/shard_map/while/body/eval_jaxpr/ppermute | solution.py:12
  219.0 7.4 collective-permute-start
  227.2 19.5 %collective-permute-start = (f32[1,2,128,128]{3,2,1,0:T(8,128)}, f32[1,2,128,128]{3,2,1,0:T(8,128)S(1)}, u32[]{:S(2)}, u32[]{:S(2)}) collective-permute-start(f32[1,2,128,128]{3,2,1,0:T(8,128)} %get-tuple-element.1762), channel_id=1, source_target_pairs={{0,1},{1,2},{2,3},{3,4},{4,5},{5,6},{6,7},{7,8},{8,9},{9,10},{10,1... | collective-permute-start | bytes 393224 | tf_op jit(solution)/shard_map/while/body/eval_jaxpr/ppermute | solution.py:12
  247.6 7.4 collective-permute-start
  255.8 11.3 %collective-permute-start = (f32[1,2,128,128]{3,2,1,0:T(8,128)}, f32[1,2,128,128]{3,2,1,0:T(8,128)S(1)}, u32[]{:S(2)}, u32[]{:S(2)}) collective-permute-start(f32[1,2,128,128]{3,2,1,0:T(8,128)} %get-tuple-element.1762), channel_id=1, source_target_pairs={{0,1},{1,2},{2,3},{3,4},{4,5},{5,6},{6,7},{7,8},{8,9},{9,10},{10,1... | collective-permute-start | bytes 393224 | tf_op jit(solution)/shard_map/while/body/eval_jaxpr/ppermute | solution.py:12
  267.9 7.4 collective-permute-start
  276.0 15.4 %collective-permute-start = (f32[1,2,128,128]{3,2,1,0:T(8,128)}, f32[1,2,128,128]{3,2,1,0:T(8,128)S(1)}, u32[]{:S(2)}, u32[]{:S(2)}) collective-permute-start(f32[1,2,128,128]{3,2,1,0:T(8,128)} %get-tuple-element.1762), channel_id=1, source_target_pairs={{0,1},{1,2},{2,3},{3,4},{4,5},{5,6},{6,7},{7,8},{8,9},{9,10},{10,1... | collective-permute-start | bytes 393224 | tf_op jit(solution)/shard_map/while/body/eval_jaxpr/ppermute | solution.py:12
  292.3 7.4 collective-permute-start
  300.4 11.3 %collective-permute-start = (f32[1,2,128,128]{3,2,1,0:T(8,128)}, f32[1,2,128,128]{3,2,1,0:T(8,128)S(1)}, u32[]{:S(2)}, u32[]{:S(2)}) collective-permute-start(f32[1,2,128,128]{3,2,1,0:T(8,128)} %get-tuple-element.1762), channel_id=1, source_target_pairs={{0,1},{1,2},{2,3},{3,4},{4,5},{5,6},{6,7},{7,8},{8,9},{9,10},{10,1... | collective-permute-start | bytes 393224 | tf_op jit(solution)/shard_map/while/body/eval_jaxpr/ppermute | solution.py:12
  312.5 7.4 collective-permute-start
  320.7 16.3 %collective-permute-start = (f32[1,2,128,128]{3,2,1,0:T(8,128)}, f32[1,2,128,128]{3,2,1,0:T(8,128)S(1)}, u32[]{:S(2)}, u32[]{:S(2)}) collective-permute-start(f32[1,2,128,128]{3,2,1,0:T(8,128)} %get-tuple-element.1762), channel_id=1, source_target_pairs={{0,1},{1,2},{2,3},{3,4},{4,5},{5,6},{6,7},{7,8},{8,9},{9,10},{10,1... | collective-permute-start | bytes 393224 | tf_op jit(solution)/shard_map/while/body/eval_jaxpr/ppermute | solution.py:12
  340.5 7.0 collective-permute-start.1
  347.8 11.7 %collective-permute-start.1 = (f32[1,2,128,128]{2,3,1,0:T(8,128)S(1)}, f32[1,2,128,128]{2,3,1,0:T(8,128)S(1)}, u32[]{:S(2)}, u32[]{:S(2)}) collective-permute-start(f32[1,2,128,128]{2,3,1,0:T(8,128)S(1)} %get-tuple-element.1774), channel_id=1, source_target_pairs={{1,0},{2,1},{3,2},{4,3},{5,4},{6,5},{7,6},{8,7},{9,8},{10,9},{11,1... | collective-permute-start | bytes 393224 | tf_op jit(solution)/shard_map/while/body/eval_jaxpr/ppermute | solution.py:12
  359.7 7.0 collective-permute-start.1
  367.0 15.8 %collective-permute-start.1 = (f32[1,2,128,128]{2,3,1,0:T(8,128)S(1)}, f32[1,2,128,128]{2,3,1,0:T(8,128)S(1)}, u32[]{:S(2)}, u32[]{:S(2)}) collective-permute-start(f32[1,2,128,128]{2,3,1,0:T(8,128)S(1)} %get-tuple-element.1774), channel_id=1, source_target_pairs={{1,0},{2,1},{3,2},{4,3},{5,4},{6,5},{7,6},{8,7},{9,8},{10,9},{11,1... | collective-permute-start | bytes 393224 | tf_op jit(solution)/shard_map/while/body/eval_jaxpr/ppermute | solution.py:12
  383.0 7.2 collective-permute-start.1
  390.4 11.6 %collective-permute-start.1 = (f32[1,2,128,128]{2,3,1,0:T(8,128)S(1)}, f32[1,2,128,128]{2,3,1,0:T(8,128)S(1)}, u32[]{:S(2)}, u32[]{:S(2)}) collective-permute-start(f32[1,2,128,128]{2,3,1,0:T(8,128)S(1)} %get-tuple-element.1774), channel_id=1, source_target_pairs={{1,0},{2,1},{3,2},{4,3},{5,4},{6,5},{7,6},{8,7},{9,8},{10,9},{11,1... | collective-permute-start | bytes 393224 | tf_op jit(solution)/shard_map/while/body/eval_jaxpr/ppermute | solution.py:12
  402.2 7.2 collective-permute-start.1
  409.6 16.6 %collective-permute-start.1 = (f32[1,2,128,128]{2,3,1,0:T(8,128)S(1)}, f32[1,2,128,128]{2,3,1,0:T(8,128)S(1)}, u32[]{:S(2)}, u32[]{:S(2)}) collective-permute-start(f32[1,2,128,128]{2,3,1,0:T(8,128)S(1)} %get-tuple-element.1774), channel_id=1, source_target_pairs={{1,0},{2,1},{3,2},{4,3},{5,4},{6,5},{7,6},{8,7},{9,8},{10,9},{11,1... | collective-permute-start | bytes 393224 | tf_op jit(solution)/shard_map/while/body/eval_jaxpr/ppermute | solution.py:12
  426.4 7.2 collective-permute-start.1
  433.8 11.6 %collective-permute-start.1 = (f32[1,2,128,128]{2,3,1,0:T(8,128)S(1)}, f32[1,2,128,128]{2,3,1,0:T(8,128)S(1)}, u32[]{:S(2)}, u32[]{:S(2)}) collective-permute-start(f32[1,2,128,128]{2,3,1,0:T(8,128)S(1)} %get-tuple-element.1774), channel_id=1, source_target_pairs={{1,0},{2,1},{3,2},{4,3},{5,4},{6,5},{7,6},{8,7},{9,8},{10,9},{11,1... | collective-permute-start | bytes 393224 | tf_op jit(solution)/shard_map/while/body/eval_jaxpr/ppermute | solution.py:12
  445.5 7.2 collective-permute-start.1
  453.0 15.7 %collective-permute-start.1 = (f32[1,2,128,128]{2,3,1,0:T(8,128)S(1)}, f32[1,2,128,128]{2,3,1,0:T(8,128)S(1)}, u32[]{:S(2)}, u32[]{:S(2)}) collective-permute-start(f32[1,2,128,128]{2,3,1,0:T(8,128)S(1)} %get-tuple-element.1774), channel_id=1, source_target_pairs={{1,0},{2,1},{3,2},{4,3},{5,4},{6,5},{7,6},{8,7},{9,8},{10,9},{11,1... | collective-permute-start | bytes 393224 | tf_op jit(solution)/shard_map/while/body/eval_jaxpr/ppermute | solution.py:12
  468.8 7.2 collective-permute-start.1
  476.2 12.3 %collective-permute-start.1 = (f32[1,2,128,128]{2,3,1,0:T(8,128)S(1)}, f32[1,2,128,128]{2,3,1,0:T(8,128)S(1)}, u32[]{:S(2)}, u32[]{:S(2)}) collective-permute-start(f32[1,2,128,128]{2,3,1,0:T(8,128)S(1)} %get-tuple-element.1774), channel_id=1, source_target_pairs={{1,0},{2,1},{3,2},{4,3},{5,4},{6,5},{7,6},{8,7},{9,8},{10,9},{11,1... | collective-permute-start | bytes 393224 | tf_op jit(solution)/shard_map/while/body/eval_jaxpr/ppermute | solution.py:12
  488.8 307.8 %collective-permute-start.1 = (f32[1,2,128,128]{2,3,1,0:T(8,128)S(1)}, f32[1,2,128,128]{2,3,1,0:T(8,128)S(1)}, u32[]{:S(2)}, u32[]{:S(2)}) collective-permute-start(f32[1,2,128,128]{2,3,1,0:T(8,128)S(1)} %get-tuple-element.1774), channel_id=1, source_target_pairs={{1,0},{2,1},{3,2},{4,3},{5,4},{6,5},{7,6},{8,7},{9,8},{10,9},{11,1... | collective-permute-start | bytes 393224 | tf_op jit(solution)/shard_map/while/body/eval_jaxpr/ppermute | solution.py:12
  817.4 7.1 collective-permute-start.1
  845.4 6.3 collective-permute-start.1
  872.3 8.0 collective-permute-start.1
  901.2 7.2 collective-permute-start.1
  929.3 5.5 collective-permute-start.1
  954.9 5.9 collective-permute-start.1
  980.5 9.9 collective-permute-start.1
  1011.3 3.2 collective-permute-start.1
  (1 other events, 2.6 us)
where the time goes:
time: 1020 us
  waiting for transfers between devices  503 us (49%)
  starting transfers between devices  221 us (22%)
  loops' own time  98.7 us (10%)
  local copies, waits for them, and re-layouts  73.3 us (7%)
  matrix products  65.1 us (6%)
  other arithmetic  55.6 us (5%)
    ppermute x46, waiting for transfers between devices, shifted(): return lax.ppermute(x, axis, pairs)  503 us
    ppermute x46, starting transfers between devices, shifted(): return lax.ppermute(x, axis, pairs)  221 us
    another operation x46, loops' own time, guarded(): lax.cond(valid, lambda: work(carried, incoming, clipped), lambda: (carrie...  94.9 us
    dot_general x128, matrix products, matmul_first(): jnp.einsum('rj,bjc->brc', table, values, precision=lax.Precision.HIGHEST)  36.4 us
    dot_general x128, matrix products, matmul_last(): jnp.einsum('bxk,kc->bxc', values, table, precision=lax.Precision.HIGHEST)  28.7 us
    dynamic_update_slice x8, local copies, waits for them, and re-layouts, backward_work(): lax.dynamic_update_slice(grad_sum, current + grad_term[0], corner_at)  27.6 us
  transfers between devices with their start and end apart: 46, of which 46 were waited for; matrix products, arithmetic and copies ran while one was open for 0% of the time, Pallas kernels for 0%

commit v1 on v0

v1 whole, which is shorter than its diff:
```python
import functools
import math

import jax
import jax.numpy as jnp
import ml_dtypes
import numpy as np
from jax import lax
from jax.experimental import pallas as pl
from jax.experimental.pallas import tpu as pltpu
from jax.sharding import PartitionSpec as P

MESH = pl.DeviceIdType.MESH


def split_table(table):
    high = table.astype(ml_dtypes.bfloat16)
    low = (table - high.astype(np.float64)).astype(ml_dtypes.bfloat16)
    return np.stack([high, low])


def right_left(matrix):
    real, imag = matrix.real, matrix.imag
    right = np.block([[real, imag], [-imag, real]])
    left = np.block([[real, -imag], [imag, real]])
    return np.stack([split_table(right), split_table(left)])


def tables(length):
    ordinal = np.arange(length)
    dft = np.exp(-2j * math.pi * (np.outer(ordinal, ordinal) % length) / length) / math.sqrt(length)
    spatial = np.where(ordinal < length // 2, ordinal, ordinal - length)
    chirp = np.exp(-1j * math.pi * (spatial * spatial % (2 * length)) / length)
    prop = (dft.conj() * chirp[None, :]) @ dft
    return np.stack([right_left(prop), right_left(dft)])


def split(values):
    high = values.astype(jnp.bfloat16)
    low = (values - high.astype(jnp.float32)).astype(jnp.bfloat16)
    return high, low


def dot(left, right):
    return jnp.dot(left, right, preferred_element_type=jnp.float32)


def two_sided(real, imag, table_ref, which):
    length = real.shape[0]
    high, low = split(jnp.concatenate([real, imag], axis=1))
    both = dot(jnp.concatenate([high, low], axis=0), table_ref[which, 0, 0])
    mid = both[:length] + both[length:] + dot(high, table_ref[which, 0, 1])
    stacked = jnp.concatenate([mid[:, :length], mid[:, length:]], axis=0)
    high, low = split(stacked)
    both = dot(table_ref[which, 1, 0], jnp.concatenate([high, low], axis=1))
    out = both[:, :length] + both[:, length:] + dot(table_ref[which, 1, 1], high)
    return out[:length], out[length:]


def complex_mul(left_real, left_imag, right_real, right_imag):
    return (
        left_real * right_real - left_imag * right_imag,
        left_real * right_imag + left_imag * right_real,
    )


def cut_kernel(offsets, ids, obj, probes, windows, start):
    positions, window = windows.shape[0], windows.shape[-1]
    side = obj.shape[-1]
    start[...] = probes[ids[lax.rem(lax.axis_index("depth"), positions)]]
    tall, wide = window + 16, 2 * window
    for position in range(positions):
        row, col = offsets[position, 0], offsets[position, 1]
        row_base = jnp.minimum((row >> 4) << 4, side - tall)
        col_base = jnp.minimum(col // window * window, side - wide)
        down, across = row - row_base, col - col_base
        down = jnp.where(down == 0, 0, tall - down)
        across = jnp.where(across == 0, 0, wide - across)
        for part in range(2):
            tile = obj[
                0, part,
                pl.ds(pl.multiple_of(row_base, 16), tall),
                pl.ds(pl.multiple_of(col_base, 128), wide),
            ].astype(jnp.float32)
            tile = pltpu.roll(tile, across, 1)[:, :window]
            windows[position, part] = pltpu.roll(tile, down, 0)[:window]


def chain_kernel(
    count, windows, start, measured, table,
    grads,
    win_in, waves, back_buf, grad_out, hop_out, hop_in,
    win_send, win_recv, grad_send, grad_recv, hop_send, hop_recv,
):
    positions, window = measured.shape[0], measured.shape[-1]
    me = lax.axis_index("depth")
    mine = lax.rem(me, positions)
    segment = me // positions
    first = segment * positions
    segments = count // positions
    last = segments - 1

    barrier = pltpu.get_barrier_semaphore()
    for step in range(1, positions):
        peer = first + lax.rem(mine + step, positions)
        pl.semaphore_signal(barrier, inc=1, device_id={"depth": peer}, device_id_type=MESH)

    @pl.when(segment < last)
    def _():
        pl.semaphore_signal(barrier, inc=1, device_id={"depth": me + positions}, device_id_type=MESH)

    @pl.when(segment > 0)
    def _():
        pl.semaphore_signal(barrier, inc=1, device_id={"depth": me - positions}, device_id_type=MESH)

    def win_copy(place):
        return pltpu.make_async_remote_copy(
            src_ref=windows.at[place], dst_ref=win_in.at[mine],
            send_sem=win_send.at[place], recv_sem=win_recv.at[mine],
            device_id={"depth": first + place}, device_id_type=MESH,
        )

    win_in[mine] = windows[mine]
    pl.semaphore_wait(
        barrier,
        positions - 1 + jnp.where(segment < last, 1, 0) + jnp.where(segment > 0, 1, 0),
    )
    for step in range(1, positions):
        win_copy(lax.rem(mine + step, positions)).start()

    def hop(which, peer):
        return pltpu.make_async_remote_copy(
            src_ref=hop_out.at[which], dst_ref=hop_in.at[which],
            send_sem=hop_send.at[which], recv_sem=hop_recv.at[which],
            device_id={"depth": peer}, device_id_type=MESH,
        )

    @pl.when(segment == 0)
    def _():
        waves[0] = start[...]

    @pl.when(segment > 0)
    def _():
        hop(0, me - positions).wait_recv()
        waves[0] = hop_in[0]

    def win_wait(slot):
        @pl.when(slot != mine)
        def _():
            pltpu.make_async_remote_copy(
                src_ref=windows.at[slot], dst_ref=win_in.at[slot],
                send_sem=win_send.at[slot], recv_sem=win_recv.at[slot],
                device_id={"depth": first + slot}, device_id_type=MESH,
            ).wait_recv()

    def exit_wave(slot):
        return complex_mul(waves[slot, 0], waves[slot, 1], win_in[slot, 0], win_in[slot, 1])

    def forward(slot, carry):
        win_wait(slot)
        real, imag = two_sided(*exit_wave(slot), table, 0)
        waves[slot + 1, 0] = real
        waves[slot + 1, 1] = imag
        return carry

    lax.fori_loop(0, positions - 1, forward, 0)
    win_wait(positions - 1)

    @pl.when(segment < last)
    def _():
        real, imag = two_sided(*exit_wave(positions - 1), table, 0)
        hop_out[0, 0] = real
        hop_out[0, 1] = imag
        hop(0, me + positions).start()
        hop(1, me + positions).wait_recv()
        back_buf[0] = hop_in[1, 0]
        back_buf[1] = hop_in[1, 1]

    @pl.when(segment == last)
    def _():
        far_real, far_imag = two_sided(*exit_wave(positions - 1), table, 1)
        excess = far_real * far_real + far_imag * far_imag - measured[mine]
        real, imag = two_sided(excess * far_real, -(excess * far_imag), table, 1)
        back_buf[0] = real
        back_buf[1] = imag

    def grad_copy(slot):
        return pltpu.make_async_remote_copy(
            src_ref=grad_out.at[slot], dst_ref=grads.at[mine],
            send_sem=grad_send.at[slot], recv_sem=grad_recv.at[mine],
            device_id={"depth": first + slot}, device_id_type=MESH,
        )

    def give(slot):
        real, imag = complex_mul(waves[slot, 0], waves[slot, 1], back_buf[0], back_buf[1])

        @pl.when(slot == mine)
        def _():
            grads[mine, 0] = real
            grads[mine, 1] = -imag

        @pl.when(slot != mine)
        def _():
            grad_out[slot, 0] = real
            grad_out[slot, 1] = -imag
            grad_copy(slot).start()

    def send_back(slot):
        return two_sided(
            *complex_mul(win_in[slot, 0], win_in[slot, 1], back_buf[0], back_buf[1]), table, 0
        )

    def backward(step, carry):
        slot = positions - 1 - step
        give(slot)
        real, imag = send_back(slot)
        back_buf[0] = real
        back_buf[1] = imag
        return carry

    lax.fori_loop(0, positions - 1, backward, 0)
    give(0)

    @pl.when(segment > 0)
    def _():
        real, imag = send_back(0)
        hop_out[1, 0] = real
        hop_out[1, 1] = imag
        hop(1, me - positions).start()
        hop(1, me - positions).wait_send()

    @pl.when(segment < last)
    def _():
        hop(0, me + positions).wait_send()

    for step in range(1, positions):
        win_copy(lax.rem(mine + step, positions)).wait_send()

    def finish(slot, carry):
        @pl.when(slot != mine)
        def _():
            grad_copy(slot).wait_send()
            pltpu.make_async_remote_copy(
                src_ref=grad_out.at[slot], dst_ref=grads.at[slot],
                send_sem=grad_send.at[slot], recv_sem=grad_recv.at[slot],
                device_id={"depth": first + slot}, device_id_type=MESH,
            ).wait_recv()

        return carry

    lax.fori_loop(0, positions, finish, 0)


def paint_kernel(offsets, grads, out, total):
    positions, window = grads.shape[0], grads.shape[-1]
    side = out.shape[-1]
    total[...] = jnp.zeros_like(total)
    tall, wide = window + 8, 2 * window
    for position in range(positions):
        row, col = offsets[position, 0], offsets[position, 1]
        row_base = jnp.minimum((row >> 3) << 3, side - tall)
        col_base = jnp.minimum(col // window * window, side - wide)
        rows = pl.ds(pl.multiple_of(row_base, 8), tall)
        cols = pl.ds(pl.multiple_of(col_base, 128), wide)
        for part in range(2):
            tile = grads[position, part]
            tile = jnp.concatenate([tile, jnp.zeros((8, window), jnp.float32)], axis=0)
            tile = pltpu.roll(tile, row - row_base, 0)
            tile = jnp.concatenate([tile, jnp.zeros((tall, window), jnp.float32)], axis=1)
            tile = pltpu.roll(tile, col - col_base, 1)
            total[part, rows, cols] += tile
    out[0] = total[...].astype(out.dtype)


def body(object_slices, probes, measured, scan_offsets, probe_ids, *, count):
    positions, window = measured.shape[0], measured.shape[-1]
    side = object_slices.shape[-1]
    assert count % positions == 0
    table = jnp.asarray(tables(window))
    vmem = pl.BlockSpec(memory_space=pltpu.VMEM)
    smem = pl.BlockSpec(memory_space=pltpu.SMEM)
    field = (2, window, window)
    stack = pltpu.VMEM((positions,) + field, jnp.float32)
    sems = pltpu.SemaphoreType.DMA((positions,))
    windows, start = pl.pallas_call(
        cut_kernel,
        out_shape=(
            jax.ShapeDtypeStruct((positions,) + field, jnp.float32),
            jax.ShapeDtypeStruct(field, jnp.float32),
        ),
        in_specs=[smem, smem, vmem, vmem],
        out_specs=(vmem, vmem),
        compiler_params=pltpu.CompilerParams(vmem_limit_bytes=16 * 1024 * 1024),
    )(scan_offsets, probe_ids, object_slices, probes)
    grads = pl.pallas_call(
        functools.partial(chain_kernel, count),
        out_shape=jax.ShapeDtypeStruct((positions,) + field, jnp.float32),
        in_specs=[vmem, vmem, vmem, vmem],
        out_specs=vmem,
        scratch_shapes=[
            stack, stack,
            pltpu.VMEM(field, jnp.float32),
            stack,
            pltpu.VMEM((2,) + field, jnp.float32),
            pltpu.VMEM((2,) + field, jnp.float32),
            sems, sems, sems, sems,
            pltpu.SemaphoreType.DMA((2,)),
            pltpu.SemaphoreType.DMA((2,)),
        ],
        compiler_params=pltpu.CompilerParams(
            collective_id=0, has_side_effects=True, vmem_limit_bytes=40 * 1024 * 1024
        ),
    )(windows, start, measured, table)
    return pl.pallas_call(
        paint_kernel,
        out_shape=jax.ShapeDtypeStruct(object_slices.shape, jnp.bfloat16),
        in_specs=[smem, vmem],
        out_specs=vmem,
        scratch_shapes=[pltpu.VMEM((2, side, side), jnp.float32)],
        compiler_params=pltpu.CompilerParams(vmem_limit_bytes=16 * 1024 * 1024),
    )(scan_offsets, grads)


def solution(mesh):
    return jax.shard_map(
        functools.partial(body, count=mesh.shape["depth"]),
        mesh=mesh,
        in_specs=(
            P(("groups", "depth"), None, None, None),
            P("groups", None, None, None),
            P("groups", None, None),
            P("groups", None),
            P("groups"),
        ),
        out_specs=P(("groups", "depth"), None, None, None),
        check_vma=False,
    )
```

time: 1020 us -> 73.1 us (0.07)
  waiting for transfers between devices: 503 us -> 0 us
  starting transfers between devices: 221 us -> 0 us
  loops' own time: 98.7 us -> 0 us
  local copies, waits for them, and re-layouts: 73.3 us -> 3.13 us
  Pallas kernels: 0 us -> 69.7 us
  matrix products: 65.1 us -> 0 us
  other arithmetic: 55.6 us -> 0 us
    ppermute x46 -> x0, waiting for transfers between devices: 503 us -> none  [shifted(): return lax.ppermute(x, axis, pairs)]
    ppermute x46 -> x0, starting transfers between devices: 221 us -> none  [shifted(): return lax.ppermute(x, axis, pairs)]
    another operation x64 -> x0, loops' own time: 98.7 us -> none  [the longest x46 94.9 us: guarded(): lax.cond(valid, lambda: work(carried, incoming, clipped), lambda: (carrie...]
    pallas_call x0 -> x3, Pallas kernels: none -> 69.7 us  [the longest x1 66 us: body(): pl.pallas_call(functools.partial(chain_kernel, count), out_shape=jax.Shap...]
    dot_general x256 -> x0, matrix products: 65.1 us -> none  [the longest x128 36.4 us: matmul_first(): jnp.einsum('rj,bjc->brc', table, values, precision=lax.Precision.HIGHEST)]
    dynamic_update_slice x8 -> x0, local copies, waits for them, and re-layouts: 27.6 us -> none  [backward_work(): lax.dynamic_update_slice(grad_sum, current + grad_term[0], corner_at)]
    convert_element_type x16 -> x0, other arithmetic: 16.5 us -> none  [the longest x8 8.26 us: forward_work(): windows = cut_windows(object_slab, corners, window).astype(jnp.float32)]
    add x32 -> x0, other arithmetic: 16.4 us -> none  [the longest x8 8.58 us: backward_work(): current + grad_term[0]]
  transfers between devices with their start and end apart: 46 -> 0, of which waited for: 46 -> 0; matrix products, arithmetic and copies ran while one was open for 0% -> 0% of each run, Pallas kernels for 0% -> 0%
where the time goes in v1:
time: 73.1 us; the launch traced here: 72.8 us
  Pallas kernels  69.7 us (95%)
  local copies, waits for them, and re-layouts  3.13 us (4%)
    pallas_call x1, Pallas kernels, body(): pl.pallas_call(functools.partial(chain_kernel, count), out_shape=jax.Shap...  66 us
    unnamed x11, local copies, waits for them, and re-layouts  3.13 us
    pallas_call x1, Pallas kernels, body(): pl.pallas_call(paint_kernel, out_shape=jax.ShapeDtypeStruct(object_slices...  2.37 us

profile of v1, /device:TPU:0, one launch (start us, length us, event | category | flops | bytes accessed | tf_op | source)
XLA Modules:
  0.0 72.8 jit_solution(13806522927622001343)
XLA Ops:
  0.0 0.0 copy-start.4
  0.0 0.8 %copy.8.offsets = s32[8,2]{1,0:T(8,128)S(1)} copy(s32[8,2]{0,1:T(2,128)} %param.9) | data formatting | bytes 128 | tf_op args[3]
  0.8 0.0 copy-done.4
  0.8 0.0 copy-start
  0.8 1.2 %copy-done = bf16[1,2,512,512]{3,2,1,0:T(8,128)(2,1)S(1)} copy-done((bf16[1,2,512,512]{3,2,1,0:T(8,128)(2,1)S(1)}, bf16[1,2,512,512]{3,2,1,0:T(8,128)(2,1)}, u32[]{:S(2)}) %copy-start) | copy-done | bytes 1048600
  2.0 0.0 copy-start.2
  2.0 1.0 %copy-done.2 = f32[4,2,128,128]{3,2,1,0:T(8,128)S(1)} copy-done((f32[4,2,128,128]{3,2,1,0:T(8,128)S(1)}, f32[4,2,128,128]{3,2,1,0:T(8,128)}, u32[]{:S(2)}) %copy-start.2) | copy-done | bytes 524312
  3.0 0.0 copy-start.1
  3.0 0.0 copy-start.3
  3.0 1.2 %shard_map.64 = (f32[8,2,128,128]{3,2,1,0:T(8,128)S(1)}, f32[2,128,128]{2,1,0:T(8,128)S(1)}) custom-call(s32[8,2]{1,0:T(8,128)S(1)} %copy.8.offsets, s32[8]{0:T(128)S(1)} %copy-done.4, bf16[1,2,512,512]{3,2,1,0:T(8,128)(2,1)S(1)} %copy-done, f32[4,2,128,128]{3,2,1,0:T(8,128)S(1)} %copy-done.2), custom_call_target="tpu_custom_call" | custom-call | tf_op jit(solution)/shard_map/pallas_call | solution.py:285
  4.3 0.0 copy-done.1
  4.3 0.1 copy-done.3
  4.4 66.0 %shard_map.65.grads = f32[8,2,128,128]{3,2,1,0:T(8,128)S(1)} custom-call(f32[8,2,128,128]{3,2,1,0:T(8,128)S(1)} %get-tuple-element.7.windows, f32[2,128,128]{2,1,0:T(8,128)S(1)} %get-tuple-element.8.start, f32[8,128,128]{2,1,0:T(8,128)S(1)} %copy-done.3, bf16[2,2,2,256,256]{4,3,2,1,0:T(8,128)(2,1)S(1)} %copy-done.1), custom_call_target="tpu_custom_call" | custom-call | tf_op jit(solution)/shard_map/pallas_call | solution.py:295
  70.5 2.4 %shard_map.66 = bf16[1,2,512,512]{3,2,1,0:T(8,128)(2,1)} custom-call(s32[8,2]{1,0:T(8,128)S(1)} %copy.8.offsets, f32[8,2,128,128]{3,2,1,0:T(8,128)S(1)} %shard_map.65.grads), custom_call_target="tpu_custom_call" | custom-call | tf_op jit(solution)/shard_map/pallas_call | solution.py:314
Async XLA Ops:
  0.0 0.8 %copy-start.4 = (s32[8]{0:T(128)S(1)}, s32[8]{0:T(128)}, u32[]{:S(2)}) copy-start(s32[8]{0:T(128)} %ids.1) | copy-start | bytes 100
  0.8 1.2 %copy-start = (bf16[1,2,512,512]{3,2,1,0:T(8,128)(2,1)S(1)}, bf16[1,2,512,512]{3,2,1,0:T(8,128)(2,1)}, u32[]{:S(2)}) copy-start(bf16[1,2,512,512]{3,2,1,0:T(8,128)(2,1)} %obj.1) | copy-start | bytes 3145732
  2.0 1.0 %copy-start.2 = (f32[4,2,128,128]{3,2,1,0:T(8,128)S(1)}, f32[4,2,128,128]{3,2,1,0:T(8,128)}, u32[]{:S(2)}) copy-start(f32[4,2,128,128]{3,2,1,0:T(8,128)} %probes.1) | copy-start | bytes 1572868
  3.0 1.3 %copy-start.1 = (bf16[2,2,2,256,256]{4,3,2,1,0:T(8,128)(2,1)S(1)}, bf16[2,2,2,256,256]{4,3,2,1,0:T(8,128)(2,1)}, u32[]{:S(2)}) copy-start(bf16[2,2,2,256,256]{4,3,2,1,0:T(8,128)(2,1)} %constant.2.clone.table) | copy-start | bytes 3145732
  3.0 1.4 %copy-start.3 = (f32[8,128,128]{2,1,0:T(8,128)S(1)}, f32[8,128,128]{2,1,0:T(8,128)}, u32[]{:S(2)}) copy-start(f32[8,128,128]{2,1,0:T(8,128)} %measured.1) | copy-start | bytes 1572868

commit v2 on v1

--- a/solution.py
+++ b/solution.py
@@ -64,33 +64,18 @@
     )
 
 
-def cut_kernel(offsets, ids, obj, probes, windows, start):
-    positions, window = windows.shape[0], windows.shape[-1]
-    side = obj.shape[-1]
-    start[...] = probes[ids[lax.rem(lax.axis_index("depth"), positions)]]
-    tall, wide = window + 16, 2 * window
-    for position in range(positions):
-        row, col = offsets[position, 0], offsets[position, 1]
-        row_base = jnp.minimum((row >> 4) << 4, side - tall)
-        col_base = jnp.minimum(col // window * window, side - wide)
-        down, across = row - row_base, col - col_base
-        down = jnp.where(down == 0, 0, tall - down)
-        across = jnp.where(across == 0, 0, wide - across)
-        for part in range(2):
-            tile = obj[
-                0, part,
-                pl.ds(pl.multiple_of(row_base, 16), tall),
-                pl.ds(pl.multiple_of(col_base, 128), wide),
-            ].astype(jnp.float32)
-            tile = pltpu.roll(tile, across, 1)[:, :window]
-            windows[position, part] = pltpu.roll(tile, down, 0)[:window]
+def one_hot(length, width, start, axis):
+    shape = (length, width) if axis == 0 else (width, length)
+    place = lax.broadcasted_iota(jnp.int32, shape, axis)
+    wanted = lax.broadcasted_iota(jnp.int32, shape, 1 - axis) + start
+    return jnp.where(place == wanted, 1.0, 0.0).astype(jnp.bfloat16)
 
 
 def chain_kernel(
-    count, windows, start, measured, table,
+    count, offsets, ids, obj, probes, measured, table_hbm,
     grads,
-    win_in, waves, back_buf, grad_out, hop_out, hop_in,
-    win_send, win_recv, grad_send, grad_recv, hop_send, hop_recv,
+    table, windows, win_in, waves, back_buf, grad_out, hop_out, hop_in,
+    win_send, win_recv, grad_send, grad_recv, hop_send, hop_recv, table_sem,
 ):
     positions, window = measured.shape[0], measured.shape[-1]
     me = lax.axis_index("depth")
@@ -100,6 +85,8 @@
     segments = count // positions
     last = segments - 1
 
+    table_copy = pltpu.make_async_copy(table_hbm, table, table_sem)
+    table_copy.start()
     barrier = pltpu.get_barrier_semaphore()
     for step in range(1, positions):
         peer = first + lax.rem(mine + step, positions)
@@ -120,13 +107,28 @@
             device_id={"depth": first + place}, device_id_type=MESH,
         )
 
-    win_in[mine] = windows[mine]
-    pl.semaphore_wait(
-        barrier,
-        positions - 1 + jnp.where(segment < last, 1, 0) + jnp.where(segment > 0, 1, 0),
-    )
-    for step in range(1, positions):
-        win_copy(lax.rem(mine + step, positions)).start()
+    side = obj.shape[-1]
+    field = obj[0].reshape(2 * side, side)
+    for pair in range(0, positions, 2):
+        places = [lax.rem(mine + pair + 1 + i, positions) for i in range(2)]
+        across = [one_hot(side, window, offsets[place, 1], 0) for place in places]
+        strips = dot(field, jnp.concatenate(across, axis=1)).astype(jnp.bfloat16)
+        for i, place in enumerate(places):
+            strip = strips[:, i * window : (i + 1) * window]
+            strip = jnp.concatenate([strip[:side], strip[side:]], axis=1)
+            tile = dot(one_hot(side, window, offsets[place, 0], 1), strip)
+            target = win_in if pair + i + 1 == positions else windows
+            target[place, 0] = tile[:, :window]
+            target[place, 1] = tile[:, window:]
+        if pair == 0:
+            pl.semaphore_wait(
+                barrier,
+                positions - 1 + jnp.where(segment < last, 1, 0) + jnp.where(segment > 0, 1, 0),
+            )
+        for i, place in enumerate(places):
+            if pair + i + 1 < positions:
+                win_copy(place).start()
+    table_copy.wait()
 
     def hop(which, peer):
         return pltpu.make_async_remote_copy(
@@ -137,7 +139,11 @@
 
     @pl.when(segment == 0)
     def _():
-        waves[0] = start[...]
+        chosen = ids[mine]
+        wave = jnp.zeros(probes.shape[1:], jnp.float32)
+        for which in range(probes.shape[0]):
+            wave = jnp.where(chosen == which, probes[which], wave)
+        waves[0] = wave
 
     @pl.when(segment > 0)
     def _():
@@ -282,23 +288,14 @@
     field = (2, window, window)
     stack = pltpu.VMEM((positions,) + field, jnp.float32)
     sems = pltpu.SemaphoreType.DMA((positions,))
-    windows, start = pl.pallas_call(
-        cut_kernel,
-        out_shape=(
-            jax.ShapeDtypeStruct((positions,) + field, jnp.float32),
-            jax.ShapeDtypeStruct(field, jnp.float32),
-        ),
-        in_specs=[smem, smem, vmem, vmem],
-        out_specs=(vmem, vmem),
-        compiler_params=pltpu.CompilerParams(vmem_limit_bytes=16 * 1024 * 1024),
-    )(scan_offsets, probe_ids, object_slices, probes)
     grads = pl.pallas_call(
         functools.partial(chain_kernel, count),
         out_shape=jax.ShapeDtypeStruct((positions,) + field, jnp.float32),
-        in_specs=[vmem, vmem, vmem, vmem],
+        in_specs=[smem, smem, vmem, vmem, vmem, pl.BlockSpec(memory_space=pl.ANY)],
         out_specs=vmem,
         scratch_shapes=[
-            stack, stack,
+            pltpu.VMEM(table.shape, jnp.bfloat16),
+            stack, stack, stack,
             pltpu.VMEM(field, jnp.float32),
             stack,
             pltpu.VMEM((2,) + field, jnp.float32),
@@ -306,11 +303,12 @@
             sems, sems, sems, sems,
             pltpu.SemaphoreType.DMA((2,)),
             pltpu.SemaphoreType.DMA((2,)),
+            pltpu.SemaphoreType.DMA,
         ],
         compiler_params=pltpu.CompilerParams(
             collective_id=0, has_side_effects=True, vmem_limit_bytes=40 * 1024 * 1024
         ),
-    )(windows, start, measured, table)
+    )(scan_offsets, probe_ids, object_slices, probes, measured, table)
     return pl.pallas_call(
         paint_kernel,
         out_shape=jax.ShapeDtypeStruct(object_slices.shape, jnp.bfloat16),

time: 73.1 us -> 75.6 us (1.034)
  local copies, waits for them, and re-layouts: 3.13 us -> 5.3 us
    unnamed x11, local copies, waits for them, and re-layouts: 3.13 us -> 5.3 us
    pallas_call x1, Pallas kernels: 66 us -> 67.6 us  [body(): pl.pallas_call(functools.partial(chain_kernel, count), out_shape=jax.Shap...]
    pallas_call x1 -> x0, Pallas kernels: 1.25 us -> none  [body(): pl.pallas_call(cut_kernel, out_shape=(jax.ShapeDtypeStruct((positions,) +...]
where the time goes in v2:
time: 75.6 us; the launch traced here: 75.3 us
  Pallas kernels  70 us (93%)
  local copies, waits for them, and re-layouts  5.3 us (7%)
    pallas_call x1, Pallas kernels, body(): pl.pallas_call(functools.partial(chain_kernel, count), out_shape=jax.Shap...  67.6 us
    unnamed x11, local copies, waits for them, and re-layouts  5.3 us
    pallas_call x1, Pallas kernels, body(): pl.pallas_call(paint_kernel, out_shape=jax.ShapeDtypeStruct(object_slices...  2.37 us

profile of v2, /device:TPU:0, one launch (start us, length us, event | category | flops | bytes accessed | tf_op | source)
XLA Modules:
  0.0 75.3 jit_solution(10554444973083646276)
XLA Ops:
  0.0 0.0 copy-start.4
  0.0 0.8 %copy.8.offsets = s32[8,2]{1,0:T(8,128)S(1)} copy(s32[8,2]{0,1:T(2,128)} %param.9) | data formatting | bytes 128 | tf_op args[3]
  0.8 0.0 copy-done.4
  0.8 0.0 copy-start
  0.8 1.2 %copy-done = bf16[1,2,512,512]{3,2,1,0:T(8,128)(2,1)S(1)} copy-done((bf16[1,2,512,512]{3,2,1,0:T(8,128)(2,1)S(1)}, bf16[1,2,512,512]{3,2,1,0:T(8,128)(2,1)}, u32[]{:S(2)}) %copy-start) | copy-done | bytes 1048600
  2.0 0.0 copy-start.1
  2.0 1.2 %copy-done.1 = bf16[2,2,2,256,256]{4,3,2,1,0:T(8,128)(2,1)S(1)} copy-done((bf16[2,2,2,256,256]{4,3,2,1,0:T(8,128)(2,1)S(1)}, bf16[2,2,2,256,256]{4,3,2,1,0:T(8,128)(2,1)}, u32[]{:S(2)}) %copy-start.1) | copy-done | bytes 1048600
  3.2 0.0 copy-start.2
  3.2 1.0 %copy-done.2 = f32[4,2,128,128]{3,2,1,0:T(8,128)S(1)} copy-done((f32[4,2,128,128]{3,2,1,0:T(8,128)S(1)}, f32[4,2,128,128]{3,2,1,0:T(8,128)}, u32[]{:S(2)}) %copy-start.2) | copy-done | bytes 524312
  4.3 0.0 copy-start.3
  4.3 1.0 %copy-done.3 = f32[8,128,128]{2,1,0:T(8,128)S(1)} copy-done((f32[8,128,128]{2,1,0:T(8,128)S(1)}, f32[8,128,128]{2,1,0:T(8,128)}, u32[]{:S(2)}) %copy-start.3) | copy-done | bytes 524312
  5.3 67.6 %shard_map.64.grads = f32[8,2,128,128]{3,2,1,0:T(8,128)S(1)} custom-call(s32[8,2]{1,0:T(8,128)S(1)} %copy.8.offsets, s32[8]{0:T(128)S(1)} %copy-done.4, bf16[1,2,512,512]{3,2,1,0:T(8,128)(2,1)S(1)} %copy-done, f32[4,2,128,128]{3,2,1,0:T(8,128)S(1)} %copy-done.2, f32[8,128,128]{2,1,0:T(8,128)S(1)} %copy-done.3, bf16[2,2,2,256,256]{4,3,2,1,0:T(8,128)(2,1)S(1)} %copy-done.1), custom_call_target="tpu_custom_call" | custom-call | tf_op jit(solution)/shard_map/pallas_call | solution.py:291
  73.0 2.4 %shard_map.65 = bf16[1,2,512,512]{3,2,1,0:T(8,128)(2,1)} custom-call(s32[8,2]{1,0:T(8,128)S(1)} %copy.8.offsets, f32[8,2,128,128]{3,2,1,0:T(8,128)S(1)} %shard_map.64.grads), custom_call_target="tpu_custom_call" | custom-call | tf_op jit(solution)/shard_map/pallas_call | solution.py:312
Async XLA Ops:
  0.0 0.8 %copy-start.4 = (s32[8]{0:T(128)S(1)}, s32[8]{0:T(128)}, u32[]{:S(2)}) copy-start(s32[8]{0:T(128)} %ids.1) | copy-start | bytes 100
  0.8 1.2 %copy-start = (bf16[1,2,512,512]{3,2,1,0:T(8,128)(2,1)S(1)}, bf16[1,2,512,512]{3,2,1,0:T(8,128)(2,1)}, u32[]{:S(2)}) copy-start(bf16[1,2,512,512]{3,2,1,0:T(8,128)(2,1)} %obj.1) | copy-start | bytes 3145732
  2.0 1.2 %copy-start.1 = (bf16[2,2,2,256,256]{4,3,2,1,0:T(8,128)(2,1)S(1)}, bf16[2,2,2,256,256]{4,3,2,1,0:T(8,128)(2,1)}, u32[]{:S(2)}) copy-start(bf16[2,2,2,256,256]{4,3,2,1,0:T(8,128)(2,1)} %constant.2.clone.table_hbm) | copy-start | bytes 3145732
  3.2 1.0 %copy-start.2 = (f32[4,2,128,128]{3,2,1,0:T(8,128)S(1)}, f32[4,2,128,128]{3,2,1,0:T(8,128)}, u32[]{:S(2)}) copy-start(f32[4,2,128,128]{3,2,1,0:T(8,128)} %probes.1) | copy-start | bytes 1572868
  4.3 1.0 %copy-start.3 = (f32[8,128,128]{2,1,0:T(8,128)S(1)}, f32[8,128,128]{2,1,0:T(8,128)}, u32[]{:S(2)}) copy-start(f32[8,128,128]{2,1,0:T(8,128)} %measured.1) | copy-start | bytes 1572868

commit v3 on v2

--- a/solution.py
+++ b/solution.py
@@ -72,43 +72,88 @@
 
 
 def chain_kernel(
-    count, offsets, ids, obj, probes, measured, table_hbm,
+    count, shift, offsets, ids, obj_hbm, probes_hbm, measured_hbm, table_hbm,
     grads,
-    table, windows, win_in, waves, back_buf, grad_out, hop_out, hop_in,
-    win_send, win_recv, grad_send, grad_recv, hop_send, hop_recv, table_sem,
+    table, obj, probes, measured, windows, win_in, waves, back_buf, grad_out, hop_out, hop_in,
+    win_send, win_recv, grad_send, grad_recv, hop_send, hop_recv, load_sem,
 ):
-    positions, window = measured.shape[0], measured.shape[-1]
+    positions, window = measured_hbm.shape[0], measured_hbm.shape[-1]
     me = lax.axis_index("depth")
     mine = lax.rem(me, positions)
     segment = me // positions
-    first = segment * positions
-    segments = count // positions
-    last = segments - 1
-
-    table_copy = pltpu.make_async_copy(table_hbm, table, table_sem)
-    table_copy.start()
+    last = count // positions - 1
+
+    loads = [
+        pltpu.make_async_copy(source, target, load_sem.at[i])
+        for i, (source, target) in enumerate((
+            (obj_hbm.at[0], obj), (table_hbm, table), (probes_hbm, probes),
+            (measured_hbm.at[mine], measured),
+        ))
+    ]
+    for load in loads:
+        load.start()
+
+    def lead(place):
+        return shift * (1 - 2 * lax.rem(place, 2))
+
+    def begin(part, place):
+        return jnp.where(part == 0, 0, part * positions - lead(place))
+
+    def holder(place):
+        return jnp.minimum(jnp.maximum(me + lead(place), 0) // positions, last)
+
+    low = begin(segment, mine)
+    slots = jnp.where(segment == last, count, begin(segment + 1, mine)) - low
+    keeps = holder(mine) == segment
+    early = (lax.rem(mine, 2) == 0) & (segment > 0)
+    held_back = jnp.where(early, shift, 0)
+
     barrier = pltpu.get_barrier_semaphore()
+
+    def greet(peer):
+        pl.semaphore_signal(barrier, inc=1, device_id={"depth": peer}, device_id_type=MESH)
+
+    def greet_owner(slot, carry):
+        @pl.when(low + slot != me)
+        def _():
+            greet(low + slot)
+
+        return carry
+
+    lax.fori_loop(0, slots, greet_owner, 0)
     for step in range(1, positions):
-        peer = first + lax.rem(mine + step, positions)
-        pl.semaphore_signal(barrier, inc=1, device_id={"depth": peer}, device_id_type=MESH)
+        place = lax.rem(mine + step, positions)
+        greet(holder(place) * positions + place)
+
+    @pl.when(jnp.logical_not(keeps))
+    def _():
+        greet(holder(mine) * positions + mine)
 
     @pl.when(segment < last)
     def _():
-        pl.semaphore_signal(barrier, inc=1, device_id={"depth": me + positions}, device_id_type=MESH)
+        greet(me + positions)
 
     @pl.when(segment > 0)
     def _():
-        pl.semaphore_signal(barrier, inc=1, device_id={"depth": me - positions}, device_id_type=MESH)
+        greet(me - positions)
+
+    greetings = (
+        slots + positions - jnp.where(keeps, 2, 0)
+        + jnp.where(segment < last, 1, 0) + jnp.where(segment > 0, 1, 0)
+    )
 
     def win_copy(place):
+        part = holder(place)
+        slot = me - begin(part, place)
         return pltpu.make_async_remote_copy(
-            src_ref=windows.at[place], dst_ref=win_in.at[mine],
-            send_sem=win_send.at[place], recv_sem=win_recv.at[mine],
-            device_id={"depth": first + place}, device_id_type=MESH,
+            src_ref=windows.at[place], dst_ref=win_in.at[slot],
+            send_sem=win_send.at[place], recv_sem=win_recv.at[slot],
+            device_id={"depth": part * positions + place}, device_id_type=MESH,
         )
 
+    loads[0].wait()
     side = obj.shape[-1]
-    field = obj[0].reshape(2 * side, side)
+    field = obj[...].reshape(2 * side, side)
     for pair in range(0, positions, 2):
         places = [lax.rem(mine + pair + 1 + i, positions) for i in range(2)]
         across = [one_hot(side, window, offsets[place, 1], 0) for place in places]
@@ -117,18 +162,24 @@
             strip = strips[:, i * window : (i + 1) * window]
             strip = jnp.concatenate([strip[:side], strip[side:]], axis=1)
             tile = dot(one_hot(side, window, offsets[place, 0], 1), strip)
-            target = win_in if pair + i + 1 == positions else windows
-            target[place, 0] = tile[:, :window]
-            target[place, 1] = tile[:, window:]
+            windows[place, 0] = tile[:, :window]
+            windows[place, 1] = tile[:, window:]
         if pair == 0:
-            pl.semaphore_wait(
-                barrier,
-                positions - 1 + jnp.where(segment < last, 1, 0) + jnp.where(segment > 0, 1, 0),
-            )
+            pl.semaphore_wait(barrier, greetings)
         for i, place in enumerate(places):
             if pair + i + 1 < positions:
                 win_copy(place).start()
-    table_copy.wait()
+
+    @pl.when(keeps)
+    def _():
+        win_in[me - low] = windows[mine]
+
+    @pl.when(jnp.logical_not(keeps))
+    def _():
+        win_copy(mine).start()
+
+    for load in loads[1:]:
+        load.wait()
 
     def hop(which, peer):
         return pltpu.make_async_remote_copy(
@@ -151,12 +202,12 @@
         waves[0] = hop_in[0]
 
     def win_wait(slot):
-        @pl.when(slot != mine)
+        @pl.when(low + slot != me)
         def _():
             pltpu.make_async_remote_copy(
-                src_ref=windows.at[slot], dst_ref=win_in.at[slot],
-                send_sem=win_send.at[slot], recv_sem=win_recv.at[slot],
-                device_id={"depth": first + slot}, device_id_type=MESH,
+                src_ref=windows.at[0], dst_ref=win_in.at[slot],
+                send_sem=win_send.at[0], recv_sem=win_recv.at[slot],
+                device_id={"depth": low + slot}, device_id_type=MESH,
             ).wait_recv()
 
     def exit_wave(slot):
@@ -169,12 +220,12 @@
         waves[slot + 1, 1] = imag
         return carry
 
-    lax.fori_loop(0, positions - 1, forward, 0)
-    win_wait(positions - 1)
+    lax.fori_loop(0, slots - 1, forward, 0)
+    win_wait(slots - 1)
 
     @pl.when(segment < last)
     def _():
-        real, imag = two_sided(*exit_wave(positions - 1), table, 0)
+        real, imag = two_sided(*exit_wave(slots - 1), table, 0)
         hop_out[0, 0] = real
         hop_out[0, 1] = imag
         hop(0, me + positions).start()
@@ -184,8 +235,8 @@
 
     @pl.when(segment == last)
     def _():
-        far_real, far_imag = two_sided(*exit_wave(positions - 1), table, 1)
-        excess = far_real * far_real + far_imag * far_imag - measured[mine]
+        far_real, far_imag = two_sided(*exit_wave(slots - 1), table, 1)
+        excess = far_real * far_real + far_imag * far_imag - measured[...]
         real, imag = two_sided(excess * far_real, -(excess * far_imag), table, 1)
         back_buf[0] = real
         back_buf[1] = imag
@@ -194,22 +245,25 @@
         return pltpu.make_async_remote_copy(
             src_ref=grad_out.at[slot], dst_ref=grads.at[mine],
             send_sem=grad_send.at[slot], recv_sem=grad_recv.at[mine],
-            device_id={"depth": first + slot}, device_id_type=MESH,
+            device_id={"depth": low + slot}, device_id_type=MESH,
         )
 
     def give(slot):
         real, imag = complex_mul(waves[slot, 0], waves[slot, 1], back_buf[0], back_buf[1])
 
-        @pl.when(slot == mine)
+        @pl.when(low + slot == me)
         def _():
             grads[mine, 0] = real
             grads[mine, 1] = -imag
 
-        @pl.when(slot != mine)
+        @pl.when(low + slot != me)
         def _():
             grad_out[slot, 0] = real
             grad_out[slot, 1] = -imag
-            grad_copy(slot).start()
+
+            @pl.when(slot >= held_back)
+            def _():
+                grad_copy(slot).start()
 
     def send_back(slot):
         return two_sided(
@@ -217,14 +271,14 @@
         )
 
     def backward(step, carry):
-        slot = positions - 1 - step
+        slot = slots - 1 - step
         give(slot)
         real, imag = send_back(slot)
         back_buf[0] = real
         back_buf[1] = imag
         return carry
 
-    lax.fori_loop(0, positions - 1, backward, 0)
+    lax.fori_loop(0, slots - 1, backward, 0)
     give(0)
 
     @pl.when(segment > 0)
@@ -239,22 +293,34 @@
     def _():
         hop(0, me + positions).wait_send()
 
-    for step in range(1, positions):
-        win_copy(lax.rem(mine + step, positions)).wait_send()
-
-    def finish(slot, carry):
-        @pl.when(slot != mine)
+    @pl.when(early)
+    def _():
+        for slot in range(shift):
+            grad_copy(slot).start()
+
+    def sent(slot, carry):
+        @pl.when(low + slot != me)
         def _():
             grad_copy(slot).wait_send()
-            pltpu.make_async_remote_copy(
-                src_ref=grad_out.at[slot], dst_ref=grads.at[slot],
-                send_sem=grad_send.at[slot], recv_sem=grad_recv.at[slot],
-                device_id={"depth": first + slot}, device_id_type=MESH,
-            ).wait_recv()
 
         return carry
 
-    lax.fori_loop(0, positions, finish, 0)
+    lax.fori_loop(0, slots, sent, 0)
+
+    def landed(place):
+        win_copy(place).wait_send()
+        pltpu.make_async_remote_copy(
+            src_ref=grad_out.at[0], dst_ref=grads.at[place],
+            send_sem=grad_send.at[0], recv_sem=grad_recv.at[place],
+            device_id={"depth": holder(place) * positions + place}, device_id_type=MESH,
+        ).wait_recv()
+
+    for step in range(1, positions):
+        landed(lax.rem(mine + step, positions))
+
+    @pl.when(jnp.logical_not(keeps))
+    def _():
+        landed(mine)
 
 
 def paint_kernel(offsets, grads, out, total):
@@ -286,24 +352,31 @@
     vmem = pl.BlockSpec(memory_space=pltpu.VMEM)
     smem = pl.BlockSpec(memory_space=pltpu.SMEM)
     field = (2, window, window)
+    shift = positions // 4
     stack = pltpu.VMEM((positions,) + field, jnp.float32)
+    chain = pltpu.VMEM((positions + shift,) + field, jnp.float32)
     sems = pltpu.SemaphoreType.DMA((positions,))
+    chain_sems = pltpu.SemaphoreType.DMA((positions + shift,))
+    hbm = pl.BlockSpec(memory_space=pltpu.HBM)
     grads = pl.pallas_call(
-        functools.partial(chain_kernel, count),
+        functools.partial(chain_kernel, count, shift),
         out_shape=jax.ShapeDtypeStruct((positions,) + field, jnp.float32),
-        in_specs=[smem, smem, vmem, vmem, vmem, pl.BlockSpec(memory_space=pl.ANY)],
+        in_specs=[smem, smem, hbm, hbm, hbm, hbm],
         out_specs=vmem,
         scratch_shapes=[
             pltpu.VMEM(table.shape, jnp.bfloat16),
-            stack, stack, stack,
+            pltpu.VMEM(object_slices.shape[1:], jnp.bfloat16),
+            pltpu.VMEM(probes.shape, jnp.float32),
+            pltpu.VMEM((window, window), jnp.float32),
+            stack, chain, chain,
             pltpu.VMEM(field, jnp.float32),
-            stack,
+            chain,
             pltpu.VMEM((2,) + field, jnp.float32),
             pltpu.VMEM((2,) + field, jnp.float32),
-            sems, sems, sems, sems,
+            sems, chain_sems, chain_sems, sems,
             pltpu.SemaphoreType.DMA((2,)),
             pltpu.SemaphoreType.DMA((2,)),
-            pltpu.SemaphoreType.DMA,
+            pltpu.SemaphoreType.DMA((4,)),
         ],
         compiler_params=pltpu.CompilerParams(
             collective_id=0, has_side_effects=True, vmem_limit_bytes=40 * 1024 * 1024

time: 75.6 us -> 72.3 us (0.956)
  Pallas kernels: 70 us -> 66.7 us
    pallas_call x1, Pallas kernels: 67.6 us -> 64.3 us  [body(): pl.pallas_call(functools.partial(chain_kernel, count, shift), out_shape=j...]
where the time goes in v3:
time: 72.3 us; the launch traced here: 72 us
  Pallas kernels  66.7 us (92%)
  local copies, waits for them, and re-layouts  5.3 us (7%)
    pallas_call x1, Pallas kernels, body(): pl.pallas_call(functools.partial(chain_kernel, count, shift), out_shape=j...  64.3 us
    unnamed x11, local copies, waits for them, and re-layouts  5.3 us
    pallas_call x1, Pallas kernels, body(): pl.pallas_call(paint_kernel, out_shape=jax.ShapeDtypeStruct(object_slices...  2.37 us

profile of v3, /device:TPU:0, one launch (start us, length us, event | category | flops | bytes accessed | tf_op | source)
XLA Modules:
  0.0 72.0 jit_solution(13066300202328162431)
XLA Ops:
  0.0 0.0 copy-start.4
  0.0 0.8 %copy.8.offsets = s32[8,2]{1,0:T(8,128)S(1)} copy(s32[8,2]{0,1:T(2,128)} %param.9) | data formatting | bytes 128 | tf_op args[3]
  0.8 0.0 copy-done.4
  0.8 0.0 copy-start
  0.8 1.2 %copy-done = bf16[1,2,512,512]{3,2,1,0:T(8,128)(2,1)S(1)} copy-done((bf16[1,2,512,512]{3,2,1,0:T(8,128)(2,1)S(1)}, bf16[1,2,512,512]{3,2,1,0:T(8,128)(2,1)}, u32[]{:S(2)}) %copy-start) | copy-done | bytes 1048600
  2.0 0.0 copy-start.1
  2.0 1.2 %copy-done.1 = bf16[2,2,2,256,256]{4,3,2,1,0:T(8,128)(2,1)S(1)} copy-done((bf16[2,2,2,256,256]{4,3,2,1,0:T(8,128)(2,1)S(1)}, bf16[2,2,2,256,256]{4,3,2,1,0:T(8,128)(2,1)}, u32[]{:S(2)}) %copy-start.1) | copy-done | bytes 1048600
  3.2 0.0 copy-start.2
  3.2 1.0 %copy-done.2 = f32[4,2,128,128]{3,2,1,0:T(8,128)S(1)} copy-done((f32[4,2,128,128]{3,2,1,0:T(8,128)S(1)}, f32[4,2,128,128]{3,2,1,0:T(8,128)}, u32[]{:S(2)}) %copy-start.2) | copy-done | bytes 524312
  4.3 0.0 copy-start.3
  4.3 1.0 %copy-done.3 = f32[8,128,128]{2,1,0:T(8,128)S(1)} copy-done((f32[8,128,128]{2,1,0:T(8,128)S(1)}, f32[8,128,128]{2,1,0:T(8,128)}, u32[]{:S(2)}) %copy-start.3) | copy-done | bytes 524312
  5.3 64.3 %shard_map.64.grads = f32[8,2,128,128]{3,2,1,0:T(8,128)S(1)} custom-call(s32[8,2]{1,0:T(8,128)S(1)} %copy.8.offsets, s32[8]{0:T(128)S(1)} %copy-done.4, bf16[1,2,512,512]{3,2,1,0:T(8,128)(2,1)S(1)} %copy-done, f32[4,2,128,128]{3,2,1,0:T(8,128)S(1)} %copy-done.2, f32[8,128,128]{2,1,0:T(8,128)S(1)} %copy-done.3, bf16[2,2,2,256,256]{4,3,2,1,0:T(8,128)(2,1)S(1)} %copy-done.1), custom_call_target="tpu_custom_call" | custom-call | tf_op jit(solution)/shard_map/pallas_call | solution.py:361
  69.6 2.4 %shard_map.65 = bf16[1,2,512,512]{3,2,1,0:T(8,128)(2,1)} custom-call(s32[8,2]{1,0:T(8,128)S(1)} %copy.8.offsets, f32[8,2,128,128]{3,2,1,0:T(8,128)S(1)} %shard_map.64.grads), custom_call_target="tpu_custom_call" | custom-call | tf_op jit(solution)/shard_map/pallas_call | solution.py:385
Async XLA Ops:
  0.0 0.8 %copy-start.4 = (s32[8]{0:T(128)S(1)}, s32[8]{0:T(128)}, u32[]{:S(2)}) copy-start(s32[8]{0:T(128)} %ids.1) | copy-start | bytes 100
  0.8 1.2 %copy-start = (bf16[1,2,512,512]{3,2,1,0:T(8,128)(2,1)S(1)}, bf16[1,2,512,512]{3,2,1,0:T(8,128)(2,1)}, u32[]{:S(2)}) copy-start(bf16[1,2,512,512]{3,2,1,0:T(8,128)(2,1)} %obj_hbm.1) | copy-start | bytes 3145732
  2.0 1.2 %copy-start.1 = (bf16[2,2,2,256,256]{4,3,2,1,0:T(8,128)(2,1)S(1)}, bf16[2,2,2,256,256]{4,3,2,1,0:T(8,128)(2,1)}, u32[]{:S(2)}) copy-start(bf16[2,2,2,256,256]{4,3,2,1,0:T(8,128)(2,1)} %constant.2.clone.table_hbm) | copy-start | bytes 3145732
  3.2 1.0 %copy-start.2 = (f32[4,2,128,128]{3,2,1,0:T(8,128)S(1)}, f32[4,2,128,128]{3,2,1,0:T(8,128)}, u32[]{:S(2)}) copy-start(f32[4,2,128,128]{3,2,1,0:T(8,128)} %probes_hbm.1) | copy-start | bytes 1572868
  4.3 1.0 %copy-start.3 = (f32[8,128,128]{2,1,0:T(8,128)S(1)}, f32[8,128,128]{2,1,0:T(8,128)}, u32[]{:S(2)}) copy-start(f32[8,128,128]{2,1,0:T(8,128)} %measured_hbm.1) | copy-start | bytes 1572868

commit v4 on v3

--- a/solution.py
+++ b/solution.py
@@ -248,22 +248,22 @@
             device_id={"depth": low + slot}, device_id_type=MESH,
         )
 
+    def keep_copy(slot):
+        return pltpu.make_async_copy(grad_out.at[slot], grads.at[mine], load_sem.at[0])
+
     def give(slot):
         real, imag = complex_mul(waves[slot, 0], waves[slot, 1], back_buf[0], back_buf[1])
 
+        grad_out[slot, 0] = real
+        grad_out[slot, 1] = -imag
+
         @pl.when(low + slot == me)
         def _():
-            grads[mine, 0] = real
-            grads[mine, 1] = -imag
-
-        @pl.when(low + slot != me)
-        def _():
-            grad_out[slot, 0] = real
-            grad_out[slot, 1] = -imag
-
-            @pl.when(slot >= held_back)
-            def _():
-                grad_copy(slot).start()
+            keep_copy(slot).start()
+
+        @pl.when((low + slot != me) & (slot >= held_back))
+        def _():
+            grad_copy(slot).start()
 
     def send_back(slot):
         return two_sided(
@@ -303,6 +303,10 @@
         def _():
             grad_copy(slot).wait_send()
 
+        @pl.when(low + slot == me)
+        def _():
+            keep_copy(slot).wait()
+
         return carry
 
     lax.fori_loop(0, slots, sent, 0)
@@ -323,12 +327,18 @@
         landed(mine)
 
 
-def paint_kernel(offsets, grads, out, total):
+def paint_kernel(offsets, grads_hbm, out_hbm, grads, out, total, load_sem, store_sem):
     positions, window = grads.shape[0], grads.shape[-1]
     side = out.shape[-1]
+    loads = [
+        pltpu.make_async_copy(grads_hbm.at[i], grads.at[i], load_sem.at[i]) for i in range(positions)
+    ]
+    for load in loads:
+        load.start()
     total[...] = jnp.zeros_like(total)
     tall, wide = window + 8, 2 * window
     for position in range(positions):
+        loads[position].wait()
         row, col = offsets[position, 0], offsets[position, 1]
         row_base = jnp.minimum((row >> 3) << 3, side - tall)
         col_base = jnp.minimum(col // window * window, side - wide)
@@ -341,7 +351,18 @@
             tile = jnp.concatenate([tile, jnp.zeros((tall, window), jnp.float32)], axis=1)
             tile = pltpu.roll(tile, col - col_base, 1)
             total[part, rows, cols] += tile
-    out[0] = total[...].astype(out.dtype)
+    pieces = store_sem.shape[0]
+    tall = side // pieces
+    stores = []
+    for piece in range(pieces):
+        rows = pl.ds(piece * tall, tall)
+        out[:, rows] = total[:, rows].astype(out.dtype)
+        stores.append(
+            pltpu.make_async_copy(out.at[:, rows], out_hbm.at[0, :, rows], store_sem.at[piece])
+        )
+        stores[-1].start()
+    for store in stores:
+        store.wait()
 
 
 def body(object_slices, probes, measured, scan_offsets, probe_ids, *, count):
@@ -349,7 +370,6 @@
     side = object_slices.shape[-1]
     assert count % positions == 0
     table = jnp.asarray(tables(window))
-    vmem = pl.BlockSpec(memory_space=pltpu.VMEM)
     smem = pl.BlockSpec(memory_space=pltpu.SMEM)
     field = (2, window, window)
     shift = positions // 4
@@ -362,7 +382,7 @@
         functools.partial(chain_kernel, count, shift),
         out_shape=jax.ShapeDtypeStruct((positions,) + field, jnp.float32),
         in_specs=[smem, smem, hbm, hbm, hbm, hbm],
-        out_specs=vmem,
+        out_specs=hbm,
         scratch_shapes=[
             pltpu.VMEM(table.shape, jnp.bfloat16),
             pltpu.VMEM(object_slices.shape[1:], jnp.bfloat16),
@@ -379,16 +399,22 @@
             pltpu.SemaphoreType.DMA((4,)),
         ],
         compiler_params=pltpu.CompilerParams(
-            collective_id=0, has_side_effects=True, vmem_limit_bytes=40 * 1024 * 1024
+            collective_id=0, has_side_effects=True, vmem_limit_bytes=58 * 1024 * 1024
         ),
     )(scan_offsets, probe_ids, object_slices, probes, measured, table)
     return pl.pallas_call(
         paint_kernel,
         out_shape=jax.ShapeDtypeStruct(object_slices.shape, jnp.bfloat16),
-        in_specs=[smem, vmem],
-        out_specs=vmem,
-        scratch_shapes=[pltpu.VMEM((2, side, side), jnp.float32)],
-        compiler_params=pltpu.CompilerParams(vmem_limit_bytes=16 * 1024 * 1024),
+        in_specs=[smem, hbm],
+        out_specs=hbm,
+        scratch_shapes=[
+            stack,
+            pltpu.VMEM((2, side, side), jnp.bfloat16),
+            pltpu.VMEM((2, side, side), jnp.float32),
+            sems,
+            pltpu.SemaphoreType.DMA((4,)),
+        ],
+        compiler_params=pltpu.CompilerParams(vmem_limit_bytes=58 * 1024 * 1024),
     )(scan_offsets, grads)
 
 

time: 72.3 us -> 69.6 us (0.963)
  local copies, waits for them, and re-layouts: 5.3 us -> 1.34 us
  Pallas kernels: 66.7 us -> 68 us
    unnamed x11 -> x1, local copies, waits for them, and re-layouts: 5.3 us -> 1.34 us
    pallas_call x1, Pallas kernels: 2.37 us -> 3.76 us  [body(): pl.pallas_call(paint_kernel, out_shape=jax.ShapeDtypeStruct(object_slices...]
where the time goes in v4:
time: 69.6 us; the launch traced here: 69.4 us
  Pallas kernels  68 us (98%)
  local copies, waits for them, and re-layouts  1.34 us (2%)
    pallas_call x1, Pallas kernels, body(): pl.pallas_call(functools.partial(chain_kernel, count, shift), out_shape=j...  64.3 us
    pallas_call x1, Pallas kernels, body(): pl.pallas_call(paint_kernel, out_shape=jax.ShapeDtypeStruct(object_slices...  3.76 us

profile of v4, /device:TPU:0, one launch (start us, length us, event | category | flops | bytes accessed | tf_op | source)
XLA Modules:
  0.0 69.4 jit_solution(153728059709550269)
XLA Ops:
  0.0 1.3 %copy.8.offsets = s32[8,2]{1,0:T(8,128)} copy(s32[8,2]{0,1:T(2,128)} %param.9) | data formatting | bytes 128 | tf_op args[3]
  1.3 64.3 %shard_map.64.grads_hbm = f32[8,2,128,128]{3,2,1,0:T(8,128)} custom-call(s32[8,2]{1,0:T(8,128)} %copy.8.offsets, s32[8]{0:T(128)} %ids.1, bf16[1,2,512,512]{3,2,1,0:T(8,128)(2,1)} %obj_hbm.1, f32[4,2,128,128]{3,2,1,0:T(8,128)} %probes_hbm.1, f32[8,128,128]{2,1,0:T(8,128)} %measured_hbm.1, bf16[2,2,2,256,256]{4,3,2,1,0:T(8,128)(2,1)} %constant.2.clone.table_hbm), custom_call_target="tpu_custom_call" | custom-call | tf_op jit(solution)/shard_map/pallas_call | solution.py:381
  65.6 3.8 %shard_map.65 = bf16[1,2,512,512]{3,2,1,0:T(8,128)(2,1)} custom-call(s32[8,2]{1,0:T(8,128)} %copy.8.offsets, f32[8,2,128,128]{3,2,1,0:T(8,128)} %shard_map.64.grads_hbm), custom_call_target="tpu_custom_call" | custom-call | tf_op jit(solution)/shard_map/pallas_call | solution.py:405

commit v5 on v4

--- a/solution.py
+++ b/solution.py
@@ -156,12 +156,12 @@
     field = obj[...].reshape(2 * side, side)
     for pair in range(0, positions, 2):
         places = [lax.rem(mine + pair + 1 + i, positions) for i in range(2)]
-        across = [one_hot(side, window, offsets[place, 1], 0) for place in places]
+        across = [one_hot(side, window, offsets[1, place], 0) for place in places]
         strips = dot(field, jnp.concatenate(across, axis=1)).astype(jnp.bfloat16)
         for i, place in enumerate(places):
             strip = strips[:, i * window : (i + 1) * window]
             strip = jnp.concatenate([strip[:side], strip[side:]], axis=1)
-            tile = dot(one_hot(side, window, offsets[place, 0], 1), strip)
+            tile = dot(one_hot(side, window, offsets[0, place], 1), strip)
             windows[place, 0] = tile[:, :window]
             windows[place, 1] = tile[:, window:]
         if pair == 0:
@@ -213,14 +213,21 @@
     def exit_wave(slot):
         return complex_mul(waves[slot, 0], waves[slot, 1], win_in[slot, 0], win_in[slot, 1])
 
-    def forward(slot, carry):
-        win_wait(slot)
+    def advance(slot):
         real, imag = two_sided(*exit_wave(slot), table, 0)
         waves[slot + 1, 0] = real
         waves[slot + 1, 1] = imag
+
+    def forward(pair, carry):
+        win_wait(2 * pair + 1)
+        win_wait(2 * pair + 2)
+        advance(2 * pair + 1)
+        advance(2 * pair + 2)
         return carry
 
-    lax.fori_loop(0, slots - 1, forward, 0)
+    win_wait(0)
+    advance(0)
+    lax.fori_loop(0, slots // 2 - 1, forward, 0)
     win_wait(slots - 1)
 
     @pl.when(segment < last)
@@ -251,12 +258,12 @@
     def keep_copy(slot):
         return pltpu.make_async_copy(grad_out.at[slot], grads.at[mine], load_sem.at[0])
 
-    def give(slot):
+    def keep_term(slot):
         real, imag = complex_mul(waves[slot, 0], waves[slot, 1], back_buf[0], back_buf[1])
-
         grad_out[slot, 0] = real
         grad_out[slot, 1] = -imag
 
+    def give(slot):
         @pl.when(low + slot == me)
         def _():
             keep_copy(slot).start()
@@ -272,13 +279,15 @@
 
     def backward(step, carry):
         slot = slots - 1 - step
-        give(slot)
+        keep_term(slot)
         real, imag = send_back(slot)
         back_buf[0] = real
         back_buf[1] = imag
+        give(slot)
         return carry
 
     lax.fori_loop(0, slots - 1, backward, 0)
+    keep_term(0)
     give(0)
 
     @pl.when(segment > 0)
@@ -339,7 +348,7 @@
     tall, wide = window + 8, 2 * window
     for position in range(positions):
         loads[position].wait()
-        row, col = offsets[position, 0], offsets[position, 1]
+        row, col = offsets[0, position], offsets[1, position]
         row_base = jnp.minimum((row >> 3) << 3, side - tall)
         col_base = jnp.minimum(col // window * window, side - wide)
         rows = pl.ds(pl.multiple_of(row_base, 8), tall)
@@ -368,7 +377,7 @@
 def body(object_slices, probes, measured, scan_offsets, probe_ids, *, count):
     positions, window = measured.shape[0], measured.shape[-1]
     side = object_slices.shape[-1]
-    assert count % positions == 0
+    assert count % positions == 0 and positions % 8 == 0
     table = jnp.asarray(tables(window))
     smem = pl.BlockSpec(memory_space=pltpu.SMEM)
     field = (2, window, window)
@@ -401,7 +410,7 @@
         compiler_params=pltpu.CompilerParams(
             collective_id=0, has_side_effects=True, vmem_limit_bytes=58 * 1024 * 1024
         ),
-    )(scan_offsets, probe_ids, object_slices, probes, measured, table)
+    )(scan_offsets.T, probe_ids, object_slices, probes, measured, table)
     return pl.pallas_call(
         paint_kernel,
         out_shape=jax.ShapeDtypeStruct(object_slices.shape, jnp.bfloat16),
@@ -415,7 +424,7 @@
             pltpu.SemaphoreType.DMA((4,)),
         ],
         compiler_params=pltpu.CompilerParams(vmem_limit_bytes=58 * 1024 * 1024),
-    )(scan_offsets, grads)
+    )(scan_offsets.T, grads)
 
 
 def solution(mesh):

time: 69.6 us -> 68.3 us (0.981)
  local copies, waits for them, and re-layouts: 1.34 us -> 0 us
    unnamed x1 -> x0, local copies, waits for them, and re-layouts: 1.34 us -> none
where the time goes in v5:
time: 68.3 us; the launch traced here: 68.1 us
  Pallas kernels  68.1 us (100%)
    pallas_call x1, Pallas kernels, body(): pl.pallas_call(functools.partial(chain_kernel, count, shift), out_shape=j...  64.3 us
    pallas_call x1, Pallas kernels, body(): pl.pallas_call(paint_kernel, out_shape=jax.ShapeDtypeStruct(object_slices...  3.73 us

profile of v5, /device:TPU:0, one launch (start us, length us, event | category | flops | bytes accessed | tf_op | source)
XLA Modules:
  0.0 68.1 jit_solution(18398357640108143106)
XLA Ops:
  0.0 64.3 %shard_map.64.grads_hbm = f32[8,2,128,128]{3,2,1,0:T(8,128)} custom-call(s32[2,8]{1,0:T(2,128)} %bitcast.1, s32[8]{0:T(128)} %ids.1, bf16[1,2,512,512]{3,2,1,0:T(8,128)(2,1)} %obj_hbm.1, f32[4,2,128,128]{3,2,1,0:T(8,128)} %probes_hbm.1, f32[8,128,128]{2,1,0:T(8,128)} %measured_hbm.1, bf16[2,2,2,256,256]{4,3,2,1,0:T(8,128)(2,1)} %constant.2.clone.table_hbm), custom_call_target="tpu_custom_call" | custom-call | tf_op jit(solution)/shard_map/pallas_call | solution.py:390
  64.3 3.7 %shard_map.65 = bf16[1,2,512,512]{3,2,1,0:T(8,128)(2,1)} custom-call(s32[2,8]{1,0:T(2,128)} %bitcast.2, f32[8,2,128,128]{3,2,1,0:T(8,128)} %shard_map.64.grads_hbm), custom_call_target="tpu_custom_call" | custom-call | tf_op jit(solution)/shard_map/pallas_call | solution.py:414

commit v6 on v5

--- a/solution.py
+++ b/solution.py
@@ -154,8 +154,27 @@
     loads[0].wait()
     side = obj.shape[-1]
     field = obj[...].reshape(2 * side, side)
+    half = positions // 2
+
+    def order(turn):
+        return 2 * lax.rem(mine // 2 + 1 + turn % half, half) + turn // half
+
+    def ship(place):
+        @pl.when(jnp.logical_not(keeps & (place == mine)))
+        def _():
+            win_copy(place).start()
+
+        @pl.when(keeps & (place == mine))
+        def _():
+            win_in[me - low] = windows[place]
+
+    def shipped(place):
+        @pl.when(jnp.logical_not(keeps & (place == mine)))
+        def _():
+            win_copy(place).wait_send()
+
     for pair in range(0, positions, 2):
-        places = [lax.rem(mine + pair + 1 + i, positions) for i in range(2)]
+        places = [order(pair), order(pair + 1)]
         across = [one_hot(side, window, offsets[1, place], 0) for place in places]
         strips = dot(field, jnp.concatenate(across, axis=1)).astype(jnp.bfloat16)
         for i, place in enumerate(places):
@@ -166,17 +185,13 @@
             windows[place, 1] = tile[:, window:]
         if pair == 0:
             pl.semaphore_wait(barrier, greetings)
-        for i, place in enumerate(places):
-            if pair + i + 1 < positions:
-                win_copy(place).start()
-
-    @pl.when(keeps)
-    def _():
-        win_in[me - low] = windows[mine]
-
-    @pl.when(jnp.logical_not(keeps))
-    def _():
-        win_copy(mine).start()
+        if pair < half:
+            for place in places:
+                ship(place)
+    for turn in range(half):
+        shipped(order(turn))
+    for turn in range(half, positions):
+        ship(order(turn))
 
     for load in loads[1:]:
         load.wait()
@@ -320,8 +335,10 @@
 
     lax.fori_loop(0, slots, sent, 0)
 
+    for turn in range(half, positions):
+        shipped(order(turn))
+
     def landed(place):
-        win_copy(place).wait_send()
         pltpu.make_async_remote_copy(
             src_ref=grad_out.at[0], dst_ref=grads.at[place],
             send_sem=grad_send.at[0], recv_sem=grad_recv.at[place],

time: 68.3 us -> 65.3 us (0.956)
  Pallas kernels: 68.1 us -> 65.1 us
    pallas_call x1, Pallas kernels: 64.3 us -> 61.4 us  [body(): pl.pallas_call(functools.partial(chain_kernel, count, shift), out_shape=j...]
where the time goes in v6:
time: 65.3 us; the launch traced here: 65.1 us
  Pallas kernels  65.1 us (100%)
    pallas_call x1, Pallas kernels, body(): pl.pallas_call(functools.partial(chain_kernel, count, shift), out_shape=j...  61.4 us
    pallas_call x1, Pallas kernels, body(): pl.pallas_call(paint_kernel, out_shape=jax.ShapeDtypeStruct(object_slices...  3.73 us

profile of v6, /device:TPU:0, one launch (start us, length us, event | category | flops | bytes accessed | tf_op | source)
XLA Modules:
  0.0 65.1 jit_solution(2958608666419437850)
XLA Ops:
  0.0 61.4 %shard_map.64.grads_hbm = f32[8,2,128,128]{3,2,1,0:T(8,128)} custom-call(s32[2,8]{1,0:T(2,128)} %bitcast.1, s32[8]{0:T(128)} %ids.1, bf16[1,2,512,512]{3,2,1,0:T(8,128)(2,1)} %obj_hbm.1, f32[4,2,128,128]{3,2,1,0:T(8,128)} %probes_hbm.1, f32[8,128,128]{2,1,0:T(8,128)} %measured_hbm.1, bf16[2,2,2,256,256]{4,3,2,1,0:T(8,128)(2,1)} %constant.2.clone.table_hbm), custom_call_target="tpu_custom_call" | custom-call | tf_op jit(solution)/shard_map/pallas_call | solution.py:407
  61.4 3.7 %shard_map.65 = bf16[1,2,512,512]{3,2,1,0:T(8,128)(2,1)} custom-call(s32[2,8]{1,0:T(2,128)} %bitcast.2, f32[8,2,128,128]{3,2,1,0:T(8,128)} %shard_map.64.grads_hbm), custom_call_target="tpu_custom_call" | custom-call | tf_op jit(solution)/shard_map/pallas_call | solution.py:431

commit v7 on v6

--- a/solution.py
+++ b/solution.py
@@ -398,7 +398,7 @@
     table = jnp.asarray(tables(window))
     smem = pl.BlockSpec(memory_space=pltpu.SMEM)
     field = (2, window, window)
-    shift = positions // 4
+    shift = 0
     stack = pltpu.VMEM((positions,) + field, jnp.float32)
     chain = pltpu.VMEM((positions + shift,) + field, jnp.float32)
     sems = pltpu.SemaphoreType.DMA((positions,))

time: 65.3 us -> 64.6 us (0.989)
  Pallas kernels: 65.1 us -> 64.4 us
    pallas_call x1, Pallas kernels: 61.4 us -> 60.7 us  [body(): pl.pallas_call(functools.partial(chain_kernel, count, shift), out_shape=j...]
where the time goes in v7:
time: 64.6 us; the launch traced here: 64.4 us
  Pallas kernels  64.4 us (100%)
    pallas_call x1, Pallas kernels, body(): pl.pallas_call(functools.partial(chain_kernel, count, shift), out_shape=j...  60.7 us
    pallas_call x1, Pallas kernels, body(): pl.pallas_call(paint_kernel, out_shape=jax.ShapeDtypeStruct(object_slices...  3.73 us

profile of v7, /device:TPU:0, one launch (start us, length us, event | category | flops | bytes accessed | tf_op | source)
XLA Modules:
  0.0 64.4 jit_solution(4855995515890042340)
XLA Ops:
  0.0 60.7 %shard_map.64.grads_hbm = f32[8,2,128,128]{3,2,1,0:T(8,128)} custom-call(s32[2,8]{1,0:T(2,128)} %bitcast.1, s32[8]{0:T(128)} %ids.1, bf16[1,2,512,512]{3,2,1,0:T(8,128)(2,1)} %obj_hbm.1, f32[4,2,128,128]{3,2,1,0:T(8,128)} %probes_hbm.1, f32[8,128,128]{2,1,0:T(8,128)} %measured_hbm.1, bf16[2,2,2,256,256]{4,3,2,1,0:T(8,128)(2,1)} %constant.2.clone.table_hbm), custom_call_target="tpu_custom_call" | custom-call | tf_op jit(solution)/shard_map/pallas_call | solution.py:407
  60.7 3.7 %shard_map.65 = bf16[1,2,512,512]{3,2,1,0:T(8,128)(2,1)} custom-call(s32[2,8]{1,0:T(2,128)} %bitcast.2, f32[8,2,128,128]{3,2,1,0:T(8,128)} %shard_map.64.grads_hbm), custom_call_target="tpu_custom_call" | custom-call | tf_op jit(solution)/shard_map/pallas_call | solution.py:431
